TPU v7x, 128 devices: a whole 4x4x4 slice. The times are simulated.
128 devices in a mesh: chan: 8 (over x, z_hi), row: 4 (over y), col: 4 (over z_lo, core).
Axes of the slice: x: 4, y: 4, z: 4 (z_hi: 2, z_lo: 2; z = z_hi * 2 + z_lo), core: 2. Of those that a mesh axis runs over, the one named last changes fastest.
Arguments:
- voltages: bfloat16 [2, 4, 512, 64, 1031], P(None, None, ('chan', 'row', 'col')), may hold values from -6 to 6
- window: float32 [8, 64], replicated, may hold values from 0.1 to 0.6
- kept_channels: int32 [48], replicated, may hold values from 0 to 63, as said below
Outputs:
- covariance: float32 [48, 2, 2048, 2048], P('chan', None, 'row', 'col')
Inputs may be any that keep to these rules, and one draw needn't show every extreme that they name: `kept_channels`: 48 distinct channel numbers of the 64-point transform, in any order.
All inputs are finite; a program needn't handle non-finite values.
Results may differ from a plain program's by a relative error of at most 0.0019.
Values may be sent and summed in bfloat16 or wider, within the bound.
No kernel may reach another device: no remote copies, remote signals or barrier semaphores. Data moves between devices by JAX's collectives and lax.ppermute only.
A program may use at most 128 MiB of HBM per device.

v0:
```python
import math

import jax
import jax.numpy as jnp
from jax import lax
from jax.sharding import Mesh
from jax.sharding import PartitionSpec as P

COL = ("col_0", "col_1")
CHAN_ROW_COL = ("chan", "row", "col_0", "col_1")
ROW_COL = ("row", "col_0", "col_1")


def in_order(tiles, dim):
    shape = list(tiles.shape[1:])
    shape[dim] *= tiles.shape[0]
    return jnp.moveaxis(tiles, 0, dim).reshape(shape)


def gather_in_order(shard, axes, turns):
    tiles = shard[None]
    for k in turns:
        tiles = lax.all_gather(tiles, axes[k], axis=0, tiled=True)
    current = [lax.axis_size(axes[k]) for k in reversed(turns)]
    tiles = tiles.reshape(*current, *shard.shape)
    turned = sorted(range(len(turns)), key=lambda place: turns[len(turns) - 1 - place])
    return tiles.transpose(*turned, *range(len(turns), tiles.ndim)).reshape(-1, *shard.shape)


def whole_of(shard, axes, turns, dim):
    return in_order(gather_in_order(shard, axes, turns), dim)


def cut_along(shard, dim, peers):
    shape = shard.shape
    tiles = shard.reshape(*shape[:dim], peers, shape[dim] // peers, *shape[dim + 1 :])
    return jnp.moveaxis(tiles, dim, 0)


def exchange_both(shard, axis, axes, splits, concats):
    sizes = [lax.axis_size(a) for a in axes]
    tiles = cut_along(shard, splits[0], sizes[0])
    tiles = jnp.moveaxis(cut_along(tiles, splits[1] + 1, sizes[1]), 0, 1)
    inside = tiles.shape[2:]
    tiles = tiles.reshape(-1, *inside)
    tiles = lax.all_to_all(tiles, axis, split_axis=0, concat_axis=0, tiled=True)
    tiles = in_order(tiles.reshape(*sizes, *inside), concats[0] + 1)
    return in_order(tiles, concats[1])


def phase_table(kept_channels, points):
    positions = jnp.arange(points, dtype=jnp.int32)
    phases = kept_channels[:, None] * positions[None, :] % points
    angles = phases.astype(jnp.float32) * (2.0 * math.pi / points)
    factor = 1.0 / math.sqrt(points)
    cosines = jnp.cos(angles) * factor
    sines = jnp.sin(angles) * factor
    return jnp.stack([jnp.stack([cosines, -sines]), jnp.stack([sines, cosines])])


def filter_bank(samples, window, frames):
    filtered = window[0][:, None] * samples[..., 0:frames]
    for tap_index in range(1, window.shape[0]):
        filtered = (
            filtered + window[tap_index][:, None] * samples[..., tap_index : tap_index + frames]
        )
    return filtered


def products(row_full, col_full):
    real_part = jnp.einsum(
        "bpmif,bpmjf->mij", row_full, col_full, preferred_element_type=jnp.float32
    )
    imag_part = jnp.einsum(
        "bmif,bmjf->mij", row_full[:, 1], col_full[:, 0], preferred_element_type=jnp.float32
    )
    imag_part = imag_part - jnp.einsum(
        "bmif,bmjf->mij", row_full[:, 0], col_full[:, 1], preferred_element_type=jnp.float32
    )
    inverse = 1.0 / (row_full.shape[0] * row_full.shape[4])
    return jnp.stack([real_part, imag_part], axis=1) * inverse


def correlate(pieces):
    row_part, col_part = pieces
    row_full = whole_of(row_part, COL, (0, 1), 0)
    col_full = lax.all_gather(col_part, "row", axis=0, tiled=True)
    return products(row_full, col_full)


def arrange(spectra, shape):
    return (spectra.reshape(shape), jnp.swapaxes(spectra, 1, 2).reshape(shape))


def shards(voltages, window, kept_channels):
    chan_count = lax.axis_size("chan")
    row_count = lax.axis_size("row")
    col_count = lax.axis_size(COL)
    points = window.shape[1]
    frames = voltages.shape[4] - window.shape[0] + 1
    slot_inputs = voltages.shape[2]
    per_chan = kept_channels.shape[0] // chan_count
    block_frames = frames // col_count
    samples = voltages.astype(jnp.float32)
    filtered = filter_bank(samples, window, frames)
    filtered = filtered.reshape(2, row_count, slot_inputs, points, col_count, block_frames)
    table = phase_table(kept_channels, points).reshape(2, 2, chan_count, per_chan, points)
    spectra = jnp.einsum(
        "qrsnbf,qpckn->crbpksf", filtered, table, precision=lax.Precision.HIGHEST
    ).astype(jnp.bfloat16)
    sectioned_shape = (
        chan_count,
        row_count * col_count,
        2,
        per_chan,
        1,
        1,
        slot_inputs,
        block_frames,
    )
    outgoing = arrange(spectra, sectioned_shape)
    arrived = (
        exchange_both(outgoing[0], CHAN_ROW_COL, ("chan", ROW_COL), (0, 1), (4, 5)),
        exchange_both(outgoing[1], CHAN_ROW_COL, ("chan", ROW_COL), (0, 1), (4, 5)),
    )
    arrived = jax.tree.map(lambda piece: piece.reshape(1, 2, per_chan, -1, block_frames), arrived)
    return correlate(arrived)


def solution(mesh):
    finer = Mesh(
        mesh.devices.reshape(mesh.shape["chan"], mesh.shape["row"], 2, 2),
        ("chan", "row", "col_0", "col_1"),
    )
    placed = (P(None, None, CHAN_ROW_COL, None, None), P(), P())
    return jax.shard_map(
        shards, mesh=finer, in_specs=placed, out_specs=P("chan", None, "row", COL), check_vma=False
    )
```

profile of v0, /device:TPU:0, one launch (start us, length us, event | category | flops | bytes accessed | tf_op | source)
XLA Modules:
  0.0 425.5 jit_solution(12734910430916442310)
XLA Ops:
  6.5 0.7 mul.173
  7.3 0.1 copy.31
  7.4 1.0 slice_bitcast_fusion.19
  8.3 0.2 fusion.31
  8.5 3.5 convert_element_type.36
  12.0 16.8 %fusion.2 = f32[2,4,4,64,1024]{4,3,2,1,0:T(8,128)} fusion(f32[2,4,4,64,1031]{4,3,2,1,0:T(8,128)S(1)} %convert_element_type.36, f32[64]{0:T(128)S(1)} %get-tuple-element.14, f32[64]{0:T(128)S(1)} %get-tuple-element.15, f32[64]{0:T(128)S(1)} %get-tuple-element.9, f32[64]{0:T(128)S(1)} %get-tuple-element.10, f32[64]{0:T(128)S(1)} %get-tuple-element.11, ...), kind=kLoop, calls=%fused_computation.4 | loop fusion | flops 31457280 | bytes 75499520 | tf_op jit(solution)/shard_map/add | solution.py:65
  28.8 10.6 %reshape.151 = f32[2,4,4,64,4,256]{5,4,3,2,1,0:T(4,128)} reshape(f32[2,4,4,64,1024]{4,3,2,1,0:T(8,128)} %fusion.2) | data formatting | bytes 16777216 | tf_op jit(solution)/shard_map/reshape | solution.py:106
  39.4 9.3 %bitcast_convert_fusion = bf16[2,8,6,4,4,4,256]{6,1,5,4,3,2,0:T(8,128)(2,1)S(1)} fusion(f32[2,4,4,64,4,256,1,1]{5,4,3,2,1,0,7,6:T(4,128)} %bitcast.102, f32[1,1,8,6,64]{4,2,0,3,1:T(8,128)S(1)} %get-tuple-element.7, f32[1,1,8,6,64]{4,2,0,3,1:T(8,128)S(1)} %get-tuple-element.6, f32[1,1,8,6,64]{4,2,0,3,1:T(8,128)S(1)} %get-tuple-element.5), kind=kOutput, calls=%fused_computation.28 | convolution fusion | flops 2417528832 | bytes 11571200 | tf_op jit(solution)/shard_map/qrsnbf,qpckn->crbpksf/dot_general | solution.py:108
  48.7 2.4 copy.33
  51.1 52.2 %all_to_all.10 = bf16[128,1,1,2,6,1,1,4,256]{8,7,4,3,6,5,2,1,0:T(4,128)(2,1)S(1)} all-to-all(bf16[128,1,1,2,6,1,1,4,256]{8,7,4,3,6,5,2,1,0:T(4,128)(2,1)S(1)} %bitcast.101), channel_id=1, replica_groups=mesh['chan'=8,'row'=4,'col_0'=2,'col_1'=2] {'chan','row','col_0','col_1'}, dimensions={0} | all-to-all | bytes 6291456 | tf_op jit(solution)/shard_map/all_to_all | solution.py:46
  103.3 3.3 copy.35
  106.6 2.2 copy.36
  108.8 79.3 %all-gather.4.cloned.1.call-done = bf16[2,1,2,6,512,256]{5,4,3,2,1,0:T(8,128)(2,1)} async-done(((bf16[1,1,2,6,512,256]{5,4,3,2,1,0:T(8,128)(2,1)}), bf16[2,1,2,6,512,256]{5,4,3,2,1,0:T(8,128)(2,1)}) %all-gather.4.cloned.1.call-update) | async-done | bytes 6291472 | tf_op jit(solution)/shard_map/all_gather | solution.py:23
  188.2 2.4 copy.38
  190.6 50.7 %all_to_all.11 = bf16[128,1,1,2,6,1,1,4,256]{8,7,4,3,6,5,2,1,0:T(4,128)(2,1)S(1)} all-to-all(bf16[128,1,1,2,6,1,1,4,256]{8,7,4,3,6,5,2,1,0:T(4,128)(2,1)S(1)} %bitcast.99), channel_id=1, replica_groups=mesh['chan'=8,'row'=4,'col_0'=2,'col_1'=2] {'chan','row','col_0','col_1'}, dimensions={0} | all-to-all | bytes 6291456 | tf_op jit(solution)/shard_map/all_to_all | solution.py:46
  241.3 1.7 copy.40
  243.1 3.0 reshape_reshape.7
  246.1 10.9 %copy.37 = bf16[2,2,1,2,6,512,256]{6,5,3,4,1,0,2:T(8,128)(2,1)} copy(bf16[2,2,1,2,6,512,256]{6,5,4,3,0,1,2:T(8,128)(2,1)} %bitcast.91) | data formatting | bytes 25165824 | tf_op jit(solution)/shard_map/transpose | solution.py:27
  257.0 104.0 %all-gather.8.cloned.1.call-done = bf16[4,2,6,512,256]{4,3,2,1,0:T(8,128)(2,1)} async-done(((bf16[1,2,6,512,256]{4,3,2,1,0:T(8,128)(2,1)}), bf16[4,2,6,512,256]{4,3,2,1,0:T(8,128)(2,1)}) %all-gather.8.cloned.1.call-update) | async-done | bytes 12582928 | tf_op jit(solution)/shard_map/all_gather | solution.py:87
  361.0 10.6 %fusion.11 = f32[6,512,512,1]{2,1,0,3:T(8,128)} fusion(bf16[4,2,6,512,256]{4,3,2,1,0:T(8,128)(2,1)} %all-gather.8.cloned.1.call-done, bf16[4,2,6,512,256]{4,3,1,2,0:T(8,128)(2,1)} %bitcast.92), kind=kOutput, calls=%fused_computation.21 | convolution fusion | flops 3221225472 | bytes 18874368 | tf_op jit(solution)/shard_map/bmif,bmjf->mij/dot_general | solution.py:77
  371.7 15.0 %fusion.16 = f32[6,1,512,512]{3,2,0,1:T(8,128)} fusion(bf16[4,2,6,512,256]{4,3,1,2,0:T(8,128)(2,1)} %bitcast.93, bf16[4,2,6,512,256]{4,3,2,1,0:T(8,128)(2,1)} %all-gather.8.cloned.1.call-done), kind=kOutput, calls=%fused_computation.29 | convolution fusion | flops 6442450944 | bytes 31457280 | tf_op jit(solution)/shard_map/bpmif,bpmjf->mij/dot_general | solution.py:71
  386.7 12.6 %fusion.13 = f32[6,1,512,512]{3,2,0,1:T(8,128)} fusion(f32[6,512,512,1]{2,1,0,3:T(8,128)} %fusion.11, bf16[4,2,6,512,256]{4,3,2,1,0:T(8,128)(2,1)} %all-gather.8.cloned.1.call-done, bf16[4,2,6,512,256]{4,3,1,2,0:T(8,128)(2,1)} %bitcast.94), kind=kOutput, calls=%fused_computation.27 | convolution fusion | flops 3222798336 | bytes 25165824 | tf_op jit(solution)/shard_map/bmif,bmjf->mij/dot_general | solution.py:74
  399.2 8.9 %maximum_multiply_fusion = f32[6,2,512,512]{3,2,0,1:T(8,128)} fusion(f32[6,1,512,512]{3,2,0,1:T(8,128)} %fusion.13, f32[6,1,512,512]{3,2,0,1:T(8,128)S(1)} %copy-done), kind=kLoop, calls=%fused_computation | loop fusion | flops 6291456 | bytes 25165824 | tf_op jit(solution)/shard_map/mul | solution.py:81
  408.1 10.9 %copy.44 = f32[6,2,512,512]{3,2,1,0:T(8,128)} copy(f32[6,2,512,512]{3,2,0,1:T(8,128)} %maximum_multiply_fusion) | data formatting | bytes 25165824 | tf_op jit(solution)/shard_map/mul | solution.py:81
  (9 shorter events, 0.2 us)
Async XLA Ops:
  6.5 181.6 %all-gather.4.cloned.1.call-start = ((), (), s32[]{:S(2)}) async-start(), calls=%async_computation.2 | async-start | bytes 9437184 | tf_op jit(solution)/shard_map/all_gather | solution.py:23
  108.8 137.3 %all-gather.6.cloned.1.call-start = ((), (), s32[]{:S(2)}) async-start(), calls=%async_computation.3 | async-start | bytes 18874368 | tf_op jit(solution)/shard_map/all_gather | solution.py:23
  188.1 172.9 %all-gather.8.cloned.1.call-start = ((), (), s32[]{:S(2)}) async-start(), calls=%async_computation.4 | async-start | bytes 15728640 | tf_op jit(solution)/shard_map/all_gather | solution.py:87
  386.7 12.6 %copy-start = (f32[6,1,512,512]{3,2,0,1:T(8,128)S(1)}, f32[6,1,512,512]{3,2,0,1:T(8,128)}, u32[]{:S(2)}) copy-start(f32[6,1,512,512]{3,2,0,1:T(8,128)} %fusion.16) | copy-start | bytes 18874372
Sparse Core Ops, SparseCore 0:
  108.9 79.1 all-gather.3
  189.8 28.5 all-gather.5
  246.2 114.7 all-gather.7
where the time goes:
time: 427 us; the launch traced here: 426 us
  waiting for transfers between devices  183 us (43%)
  blocking collectives  103 us (24%)
  local copies, waits for them, and re-layouts  49.2 us (12%)
  matrix products  47.5 us (11%)
  other arithmetic  29.4 us (7%)
  between operations  13.2 us (3%)
    all_gather x1, waiting for transfers between devices, correlate(): col_full = lax.all_gather(col_part, 'row', axis=0, tiled=True)  104 us
    all_to_all x2, blocking collectives, exchange_both(): tiles = lax.all_to_all(tiles, axis, split_axis=0, concat_axis=0, tiled=True)  103 us
    all_gather x2, waiting for transfers between devices, gather_in_order(): tiles = lax.all_gather(tiles, axes[k], axis=0, tiled=True)  79.3 us
    add x1, other arithmetic, filter_bank(): filtered + window[tap_index][:, None] * samples[..., tap_index:tap_index...  16.8 us
    dot_general x1, matrix products, products(): jnp.einsum('bpmif,bpmjf->mij', row_full, col_full, preferred_element_type...  15 us
    dot_general x1, matrix products, products(): jnp.einsum('bmif,bmjf->mij', row_full[:, 1], col_full[:, 0], preferred_el...  12.6 us
    transpose x1, local copies, waits for them, and re-layouts, gather_in_order(): tiles.transpose(*turned, *range(len(turns), tiles.ndim))  10.9 us
    mul x1, local copies, waits for them, and re-layouts, products(): return jnp.stack([real_part, imag_part], axis=1) * inverse  10.9 us
  transfers between devices with their start and end apart: 3, of which 2 were waited for; matrix products, arithmetic and copies ran while one was open for 4% of the time, Pallas kernels for 0%

commit v1 on v0

v1 whole, which is shorter than its diff:
```python
import functools
import math

import jax
import jax.numpy as jnp
from jax import lax
from jax.experimental import pallas as pl
from jax.experimental.pallas import tpu as pltpu
from jax.sharding import Mesh
from jax.sharding import PartitionSpec as P

CHAN_COL = ("chan", "col_0", "col_1")
CHAN_ROW_COL = ("chan", "row", "col_0", "col_1")
CHUNKS = 2
STEPS = (("row", (0,)), ("col", (0,)), ("row", (1,)), ("col", (1,)))
F32 = jnp.float32
BF16 = jnp.bfloat16


def split_bf16(x):
    hi = x.astype(BF16)
    return hi, (x - hi.astype(F32)).astype(BF16)


def phase_rows(kept_channels, points, chan_count, slots):
    positions = jnp.arange(points, dtype=jnp.int32)
    phases = kept_channels[:, None] * positions[None, :] % points
    angles = phases.astype(F32) * (2.0 * math.pi / points)
    factor = 1.0 / math.sqrt(points)
    cosines = jnp.cos(angles) * factor
    sines = jnp.sin(angles) * factor
    per_chan = kept_channels.shape[0] // chan_count
    real = jnp.concatenate([cosines, sines], axis=1)
    imag = jnp.concatenate([-sines, cosines], axis=1)
    rows = jnp.stack([real, imag], axis=1)
    rows = rows.reshape(chan_count, CHUNKS, per_chan // CHUNKS, 2, 2 * points)
    rows = rows.transpose(1, 0, 2, 3, 4).reshape(-1, 2 * points)
    eye = jnp.eye(slots, dtype=F32)
    blocks = rows[:, None, None, :] * eye[None, :, :, None]
    blocks = blocks.reshape(rows.shape[0] * slots, slots * 2 * points)
    near = lax.reduce_precision(blocks, 8, 7)
    return near.astype(BF16), (blocks - near).astype(BF16)


def spectra_kernel(volt_ref, win_ref, hi_ref, lo_ref, *refs):
    out_refs, part_ref = refs[:-1], refs[-1]
    slots, points, _ = volt_ref.shape[2:]
    frames = part_ref.shape[1]
    depth = slots * 2 * points
    group = 16
    steps = points // group

    def filter_rows(i, _):
        slot, plane, at = i // (2 * steps), i // steps % 2, i % steps * group
        x = volt_ref[plane, 0, slot, pl.ds(at, group), :]
        total = None
        for tap in range(win_ref.shape[0]):
            gain = win_ref[tap, pl.ds(at, group), :]
            gain = jnp.concatenate([gain] * (frames // 128), axis=1)
            term = gain * x[:, tap : tap + frames].astype(F32)
            total = term if total is None else total + term
        hi, lo = split_bf16(total)
        to = pl.multiple_of(i * group, group)
        part_ref[pl.ds(to, group)] = hi
        part_ref[pl.ds(to + depth, group)] = lo
        return 0

    lax.fori_loop(0, slots * 2 * steps, filter_rows, 0, unroll=4)
    out = jnp.dot(hi_ref[...], part_ref[0:depth], preferred_element_type=F32)
    out = out + jnp.dot(hi_ref[...], part_ref[depth:], preferred_element_type=F32)
    out = out + jnp.dot(lo_ref[...], part_ref[0:depth], preferred_element_type=F32)
    chans = out_refs[0].shape[0]
    out = out.astype(BF16).reshape(CHUNKS, chans, -1, frames)
    rows = out.shape[2]
    for (kind, pieces), ref in zip(STEPS, out_refs):
        for k, piece in enumerate(pieces):
            at = slice(k * rows, (k + 1) * rows)
            if kind == "col":
                ref[:, 0, at] = out[piece]
                continue
            quarter = ref.shape[4]
            for part in range(frames // quarter):
                ref[:, 0, part, at] = out[piece, :, :, part * quarter : (part + 1) * quarter]


def spectra(voltages, window, hi, lo, chan_count, col_count):
    _, panels, slots, points, blocks = voltages.shape
    taps = window.shape[0]
    frames = blocks - taps + 1
    rows = hi.shape[0] // (CHUNKS * chan_count)
    depth = hi.shape[1]
    width = pl.cdiv(blocks, 128) * 128
    window = jnp.broadcast_to(window[:, :, None], (taps, points, 128))
    quarter = frames // col_count
    specs, shapes = [], []
    for kind, pieces in STEPS:
        high = rows * len(pieces)
        inner = (high, frames) if kind == "col" else (col_count, high, quarter)
        zeros = (0,) * len(inner)
        specs.append(
            pl.BlockSpec((chan_count, 1, *inner), lambda p, zeros=zeros: (0, p, *zeros))
        )
        shapes.append(jax.ShapeDtypeStruct((chan_count, panels, *inner), BF16))
    return pl.pallas_call(
        spectra_kernel,
        grid=(panels,),
        in_specs=[
            pl.BlockSpec((2, 1, slots, points, width), lambda p: (0, p, 0, 0, 0)),
            pl.BlockSpec((taps, points, 128), lambda p: (0, 0, 0)),
            pl.BlockSpec(hi.shape, lambda p: (0, 0)),
            pl.BlockSpec(lo.shape, lambda p: (0, 0)),
        ],
        out_specs=specs,
        out_shape=shapes,
        scratch_shapes=[pltpu.VMEM((2 * depth, frames), BF16)],
        compiler_params=pltpu.CompilerParams(vmem_limit_bytes=48 << 20),
        name="spectra",
    )(voltages, window, hi, lo)


def regroup_kernel(size, slots, x_ref, *out_refs):
    kinds = out_refs[0].shape[0]
    total = kinds * len(out_refs)
    per = size // total
    rows = lax.broadcasted_iota(jnp.int32, (size, size), 0)
    cols = lax.broadcasted_iota(jnp.int32, (size, size), 1)
    kind, rest = rows // per, rows % per
    source = (rest // slots) * (total * slots) + kind * slots + rest % slots
    pick = (cols == source).astype(F32).astype(BF16)
    for g in range(x_ref.shape[0] // size):
        out = jnp.dot(
            pick, x_ref[g * size : (g + 1) * size], preferred_element_type=F32
        ).astype(BF16)
        out = out.reshape(total, per, -1)
        for k, ref in enumerate(out_refs):
            ref[:, g * per : (g + 1) * per] = out[k * kinds : (k + 1) * kinds]


def regroup(x, kinds, slots):
    count, rows, frames = x.shape
    pieces = rows // (kinds * slots)
    size = rows * (16 if pieces == 1 else 8)
    steps = 2
    part = count * rows // steps
    high = count * slots
    return pl.pallas_call(
        functools.partial(regroup_kernel, size, slots),
        grid=(steps,),
        in_specs=[pl.BlockSpec((part, frames), lambda g: (g, 0))],
        out_specs=[pl.BlockSpec((kinds, high // steps, frames), lambda g: (0, g, 0))] * pieces,
        out_shape=[jax.ShapeDtypeStruct((kinds, high, frames), BF16)] * pieces,
        cost_estimate=pl.CostEstimate(
            flops=2 * size * count * rows * frames,
            bytes_accessed=4 * count * rows * frames,
            transcendentals=0,
        ),
        compiler_params=pltpu.CompilerParams(vmem_limit_bytes=24 << 20),
        name="regroup",
    )(x.reshape(count * rows, frames))


def correlate_kernel(order_ref, *refs):
    cols, pieces = refs[0:4], refs[4:8]
    out_ref, a_ref, b_ref = refs[-3:]
    frames = cols[0].shape[4]
    quarter = pieces[0].shape[3]
    for plane in range(2):
        for k, ref in enumerate(cols):
            b_ref[:, order_ref[k], :, plane * frames : (plane + 1) * frames] = ref[0, plane]
        for k, ref in enumerate(pieces):
            at = pl.multiple_of(order_ref[4 + k] * quarter, quarter)
            part = ref[0, plane]
            a_ref[:, pl.ds(plane * frames + at, quarter)] = part
            if plane == 0:
                a_ref[:, pl.ds(2 * frames + at, quarter)] = -part
    size = a_ref.shape[0]
    b = b_ref[...].reshape(size, 2 * frames)
    scale = 1.0 / frames
    for plane in range(2):
        a = a_ref[:, plane * frames : (plane + 2) * frames]
        out_ref[0, plane] = (
            lax.dot_general(a, b, (((1,), (1,)), ((), ())), preferred_element_type=F32) * scale
        )


def correlate(order, cols, pieces, out, chunk, total):
    channels, _, size, quarter = pieces[0].shape
    _, _, chans, rows_of, frames = cols[0].shape
    col_spec = pl.BlockSpec((1, 2, chans, rows_of, frames), lambda k, s: (k, 0, 0, 0, 0))
    row_spec = pl.BlockSpec((1, 2, size, quarter), lambda k, s: (k, 0, 0, 0))
    in_specs = [col_spec] * 4 + [row_spec] * 4
    operands = [order, *cols, *pieces]
    aliases = {}
    if out is not None:
        in_specs.append(pl.BlockSpec(memory_space=pl.ANY))
        aliases = {len(operands): 0}
        operands.append(out)
    first = chunk * channels
    return pl.pallas_call(
        correlate_kernel,
        grid_spec=pltpu.PrefetchScalarGridSpec(
            num_scalar_prefetch=1,
            grid=(channels,),
            in_specs=in_specs,
            out_specs=pl.BlockSpec((1, 2, size, size), lambda k, s: (first + k, 0, 0, 0)),
            scratch_shapes=[
                pltpu.VMEM((size, 3 * frames), BF16),
                pltpu.VMEM((chans, 4, rows_of, 2 * frames), BF16),
            ],
        ),
        out_shape=jax.ShapeDtypeStruct((total, 2, size, size), F32),
        input_output_aliases=aliases,
        compiler_params=pltpu.CompilerParams(vmem_limit_bytes=48 << 20),
        cost_estimate=pl.CostEstimate(
            flops=8 * channels * size * size * frames,
            bytes_accessed=channels * (8 * size * frames + 8 * size * size),
            transcendentals=0,
        ),
        name="correlate",
    )(*operands)


def shards(voltages, window, kept_channels):
    chan_count = lax.axis_size("chan")
    row_count = lax.axis_size("row")
    col_count = 4
    points = window.shape[1]
    slots = voltages.shape[2]
    per_chan = kept_channels.shape[0] // chan_count
    hi, lo = phase_rows(kept_channels, points, chan_count, slots)
    sent = spectra(voltages, window, hi, lo, chan_count, col_count)
    kinds = per_chan // CHUNKS * 2
    me, far, near = (lax.axis_index(a) for a in ("row", "col_0", "col_1"))
    order = [(me + k) % row_count for k in (0, row_count - 1, 1, 2)]
    order += [f * 2 + n for f, n in ((far, near), (1 - far, near), (far, 1 - near), (1 - far, 1 - near))]
    order = jnp.stack(order).astype(jnp.int32)

    def turn(x, by):
        return lax.ppermute(x, "row", [(k, (k + by) % row_count) for k in range(row_count)])

    def swap(x, axis):
        return lax.ppermute(x, axis, [(0, 1), (1, 0)])

    cols, rows = [None] * CHUNKS, [None] * CHUNKS
    token = None
    for (kind, pieces), block in zip(STEPS, sent):
        axes = CHAN_COL if kind == "col" else CHAN_ROW_COL
        block = block.reshape(-1, *block.shape[-2:])
        if token is not None:
            block, token = lax.optimization_barrier((block, token))
        block = lax.all_to_all(block, axes, split_axis=0, concat_axis=0, tiled=True)
        block = regroup(block, kinds, slots)
        token = block[0]
        for piece, part in zip(pieces, block):
            if kind == "col":
                parts = [part, turn(part, 1), turn(part, -1), turn(part, 2)]
                parts = [c.reshape(kinds // 2, 2, chan_count, -1, c.shape[2]) for c in parts]
                cols[piece] = parts
            else:
                parts = [part, swap(part, "col_0")]
                parts += [swap(r, "col_1") for r in parts]
                rows[piece] = [r.reshape(kinds // 2, 2, *r.shape[1:]) for r in parts]
    out = None
    for chunk in range(CHUNKS):
        out = correlate(order, cols[chunk], rows[chunk], out, chunk, per_chan)
    return out


def solution(mesh):
    finer = Mesh(
        mesh.devices.reshape(mesh.shape["chan"], mesh.shape["row"], 2, 2),
        ("chan", "row", "col_0", "col_1"),
    )
    placed = (P(None, None, CHAN_ROW_COL, None, None), P(), P())
    return jax.shard_map(
        shards,
        mesh=finer,
        in_specs=placed,
        out_specs=P("chan", None, "row", ("col_0", "col_1")),
        check_vma=False,
    )
```

time: 427 us -> 278 us (0.65)
  Pallas kernels: 0 us -> 51.4 us
  matrix products: 47.5 us -> 0 us
  waiting for transfers between devices: 183 us -> 137 us
  local copies, waits for them, and re-layouts: 49.2 us -> 6.19 us
  blocking collectives: 103 us -> 61.4 us
  other arithmetic: 29.4 us -> 0.58 us
  starting transfers between devices: 0.08 us -> 20.2 us
  between operations: 13.2 us -> 0.15 us
    all_gather x3 -> x0, waiting for transfers between devices: 183 us -> none  [the longest x1 104 us: correlate(): col_full = lax.all_gather(col_part, 'row', axis=0, tiled=True)]
    ppermute x0 -> x12, waiting for transfers between devices: none -> 110 us  [the longest x6 78.3 us: turn(): lax.ppermute(x, 'row', [(k, (k + by) % row_count) for k in range(row_coun...]
    pallas_call x0 -> x7, Pallas kernels: none -> 51.4 us  [the longest x2 25.2 us: correlate(): pl.pallas_call(correlate_kernel, grid_spec=pltpu.PrefetchScalarGridSpec(n...]
    dot_general x4 -> x0, matrix products: 47.5 us -> none  [the longest x1 15 us: products(): jnp.einsum('bpmif,bpmjf->mij', row_full, col_full, preferred_element_type...]
    all_to_all x2, blocking collectives: 103 us -> 61.4 us  [shards(): block = lax.all_to_all(block, axes, split_axis=0, concat_axis=0, tiled=True)]
    all_to_all x0 -> x2, waiting for transfers between devices: none -> 26.9 us  [shards(): block = lax.all_to_all(block, axes, split_axis=0, concat_axis=0, tiled=True)]
    add x1 -> x0, other arithmetic: 16.8 us -> none  [filter_bank(): filtered + window[tap_index][:, None] * samples[..., tap_index:tap_index...]
    reshape x2 -> x0, local copies, waits for them, and re-layouts: 13.8 us -> none  [the longest x1 10.6 us: shards(): filtered.reshape(2, row_count, slot_inputs, points, col_count, block_frames)]
  transfers between devices with their start and end apart: 3 -> 14, of which waited for: 2 -> 6; matrix products, arithmetic and copies ran while one was open for 4% -> 0% of each run, Pallas kernels for 0% -> 5%
where the time goes in v1:
time: 278 us; the launch traced here: 277 us
  waiting for transfers between devices  137 us (49%)
  blocking collectives  61.4 us (22%)
  Pallas kernels  51.4 us (18%)
  starting transfers between devices  20.2 us (7%)
  local copies, waits for them, and re-layouts  6.19 us (2%)
    ppermute x6, waiting for transfers between devices, turn(): lax.ppermute(x, 'row', [(k, (k + by) % row_count) for k in range(row_coun...  78.3 us
    all_to_all x2, blocking collectives, shards(): block = lax.all_to_all(block, axes, split_axis=0, concat_axis=0, tiled=True)  61.4 us
    ppermute x6, waiting for transfers between devices, swap(): return lax.ppermute(x, axis, [(0, 1), (1, 0)])  31.9 us
    all_to_all x2, waiting for transfers between devices, shards(): block = lax.all_to_all(block, axes, split_axis=0, concat_axis=0, tiled=True)  26.9 us
    pallas_call x2, Pallas kernels, correlate(): pl.pallas_call(correlate_kernel, grid_spec=pltpu.PrefetchScalarGridSpec(n...  25.2 us
    pallas_call x1, Pallas kernels, spectra(): pl.pallas_call(spectra_kernel, grid=(panels,), in_specs=[pl.BlockSpec((2,...  20.3 us
    all_to_all x2, starting transfers between devices, shards(): block = lax.all_to_all(block, axes, split_axis=0, concat_axis=0, tiled=True)  8.78 us
    ppermute x6, starting transfers between devices, turn(): lax.ppermute(x, 'row', [(k, (k + by) % row_count) for k in range(row_coun...  8.74 us
  transfers between devices with their start and end apart: 14, of which 6 were waited for; matrix products, arithmetic and copies ran while one was open for 0% of the time, Pallas kernels for 5%

profile of v1, /device:TPU:0, one launch (start us, length us, event | category | flops | bytes accessed | tf_op | source)
XLA Modules:
  0.0 277.1 jit_solution(2243942982981329175)
XLA Ops:
  1.6 20.3 %spectra.1 = (bf16[8,4,4,24,256]{4,3,2,1,0:T(8,128)(2,1)S(1)}, bf16[8,4,24,1024]{3,2,1,0:T(8,128)(2,1)S(1)}, bf16[8,4,4,24,256]{4,3,2,1,0:T(8,128)(2,1)S(1)}, bf16[8,4,24,1024]{3,2,1,0:T(8,128)(2,1)}) custom-call(bf16[2,4,4,64,1031]{4,3,2,1,0:T(8,128)(2,1)} %volt_ref.1, f32[8,64,128]{2,1,0:T(8,128)S(1)} %broadcast_in_dim.2.win_ref, ...), custom_call_target="tpu_custom_call" | custom-call | tf_op jit(solution)/shard_map/spectra/pallas_call | solution.py:104
  21.9 35.2 %all_to_all.20 = bf16[128,24,256]{2,1,0:T(8,128)(2,1)S(1)} all-to-all(bf16[128,24,256]{2,1,0:T(8,128)(2,1)S(1)} %bitcast.49), channel_id=1, replica_groups=mesh['chan'=8,'row'=4,'col_0'=2,'col_1'=2] {'chan','row','col_0','col_1'}, dimensions={0} | all-to-all | bytes 3145728 | tf_op jit(solution)/shard_map/all_to_all | solution.py:251
  57.1 2.1 regroup.4
  59.2 26.2 %all_to_all.21 = bf16[32,24,1024]{2,1,0:T(8,128)(2,1)S(1)} all-to-all(bf16[32,24,1024]{2,1,0:T(8,128)(2,1)S(1)} %bitcast.48), channel_id=1, replica_groups=mesh['chan'=8,'row'=4,'col_0'=2,'col_1'=2] {'chan','col_0','col_1'}, dimensions={0} | all-to-all | bytes 3145728 | tf_op jit(solution)/shard_map/all_to_all | solution.py:251
  85.4 1.3 regroup.5
  87.9 4.7 %all-to-all-start.2 = ((bf16[128,24,256]{2,1,0:T(8,128)(2,1)}), bf16[128,24,256]{2,1,0:T(8,128)(2,1)S(1)}, u32[]{:S(2)}, u32[]{:S(2)}) async-start(bf16[128,24,256]{2,1,0:T(8,128)(2,1)} %bitcast.47), calls=%async_computation.2 | async-start | bytes 3145728 | tf_op jit(solution)/shard_map/all_to_all | solution.py:251
  93.8 23.1 %all-to-all-done.2 = bf16[128,24,256]{2,1,0:T(8,128)(2,1)S(1)} async-done(((bf16[128,24,256]{2,1,0:T(8,128)(2,1)}), bf16[128,24,256]{2,1,0:T(8,128)(2,1)S(1)}, u32[]{:S(2)}, u32[]{:S(2)}) %all-to-all-start.2) | async-done | bytes 1572896 | tf_op jit(solution)/shard_map/all_to_all | solution.py:251
  116.9 1.3 regroup.6
  118.2 4.0 %all-to-all-start.3 = ((bf16[32,24,1024]{2,1,0:T(8,128)(2,1)}), bf16[32,24,1024]{2,1,0:T(8,128)(2,1)S(1)}, u32[]{:S(2)}, u32[]{:S(2)}) async-start(bf16[32,24,1024]{2,1,0:T(8,128)(2,1)} %bitcast.51), calls=%async_computation.3 | async-start | bytes 3145728 | tf_op jit(solution)/shard_map/all_to_all | solution.py:251
  122.2 1.8 collective-permute-start.8
  124.1 1.6 collective-permute-start.7
  126.1 31.9 %collective-permute-done.9 = bf16[6,512,256]{2,1,0:T(8,128)(2,1)} collective-permute-done((bf16[6,512,256]{2,1,0:T(8,128)(2,1)}, bf16[6,512,256]{2,1,0:T(8,128)(2,1)}, u32[]{:S(2)}, u32[]{:S(2)}) %collective-permute-start.9) | collective-permute-done | bytes 1572896 | tf_op jit(solution)/shard_map/ppermute | solution.py:242
  158.0 1.3 collective-permute-start.3
  159.4 3.8 %all-to-all-done.3 = bf16[32,24,1024]{2,1,0:T(8,128)(2,1)S(1)} async-done(((bf16[32,24,1024]{2,1,0:T(8,128)(2,1)}), bf16[32,24,1024]{2,1,0:T(8,128)(2,1)S(1)}, u32[]{:S(2)}, u32[]{:S(2)}) %all-to-all-start.3) | async-done | bytes 1572896 | tf_op jit(solution)/shard_map/all_to_all | solution.py:251
  164.3 1.4 copy-done.2
  165.7 1.3 regroup.7
  167.2 25.7 %collective-permute-done.7 = bf16[6,128,1024]{2,1,0:T(8,128)(2,1)} collective-permute-done((bf16[6,128,1024]{2,1,0:T(8,128)(2,1)}, bf16[6,128,1024]{2,1,0:T(8,128)(2,1)}, u32[]{:S(2)}, u32[]{:S(2)}) %collective-permute-start.7) | collective-permute-done | bytes 1572896 | tf_op jit(solution)/shard_map/ppermute | solution.py:239
  192.8 2.9 %collective-permute-start.2 = (bf16[6,128,1024]{2,1,0:T(8,128)(2,1)S(1)}, bf16[6,128,1024]{2,1,0:T(8,128)(2,1)}, u32[]{:S(2)}, u32[]{:S(2)}) collective-permute-start(bf16[6,128,1024]{2,1,0:T(8,128)(2,1)S(1)} %regroup.7), channel_id=1, source_target_pairs={{0,8},{4,12},{8,0},{12,4},{1,9},{5,13},{9,1},{13,5},{2,10},{6,14},... | collective-permute-start | bytes 4718600 | tf_op jit(solution)/shard_map/ppermute | solution.py:239
  195.7 1.5 collective-permute-start.1
  197.8 1.4 copy-done.4
  199.2 12.6 %correlate.2.refs_8_ = f32[6,2,512,512]{3,2,1,0:T(8,128)} custom-call(s32[8]{0:T(128)S(1)} %stack.40.order_ref, bf16[3,2,8,16,1024]{4,3,2,1,0:T(8,128)(2,1)S(1)} %bitcast.46, bf16[3,2,8,16,1024]{4,3,2,1,0:T(8,128)(2,1)} %bitcast.27.refs_1_, bf16[3,2,8,16,1024]{4,3,2,1,0:T(8,128)(2,1)} %bitcast.28.refs_2_, bf16[3,2,8,16,1024]{4,3,2,1,0:T(8,128)(2,1)} %bitcast.29.refs_3_, ...), custom_call_target="tpu_custom_call" | custom-call | flops 6442450944 | bytes 18874368 | tf_op jit(solution)/shard_map/correlate/pallas_call | solution.py:199
  211.8 20.0 %collective-permute-done.2 = bf16[6,128,1024]{2,1,0:T(8,128)(2,1)} collective-permute-done((bf16[6,128,1024]{2,1,0:T(8,128)(2,1)S(1)}, bf16[6,128,1024]{2,1,0:T(8,128)(2,1)}, u32[]{:S(2)}, u32[]{:S(2)}) %collective-permute-start.2) | collective-permute-done | bytes 1572896 | tf_op jit(solution)/shard_map/ppermute | solution.py:239
  231.8 32.6 %collective-permute-done.1 = bf16[6,128,1024]{2,1,0:T(8,128)(2,1)} collective-permute-done((bf16[6,128,1024]{2,1,0:T(8,128)(2,1)S(1)}, bf16[6,128,1024]{2,1,0:T(8,128)(2,1)}, u32[]{:S(2)}, u32[]{:S(2)}) %collective-permute-start.1) | collective-permute-done | bytes 1572896 | tf_op jit(solution)/shard_map/ppermute | solution.py:239
  264.5 12.6 %correlate.3 = f32[6,2,512,512]{3,2,1,0:T(8,128)} custom-call(s32[8]{0:T(128)S(1)} %stack.40.order_ref, bf16[3,2,8,16,1024]{4,3,2,1,0:T(8,128)(2,1)S(1)} %bitcast.41, bf16[3,2,8,16,1024]{4,3,2,1,0:T(8,128)(2,1)} %bitcast.19.refs_1_, bf16[3,2,8,16,1024]{4,3,2,1,0:T(8,128)(2,1)} %bitcast.20.refs_2_, ...), custom_call_target="tpu_custom_call", output_to_operand_aliasing={{}: (9, {})} | custom-call | flops 6442450944 | bytes 18874368 | tf_op jit(solution)/shard_map/correlate/pallas_call | solution.py:199
  (37 shorter events, 6.3 us)
Async XLA Ops:
  0.0 1.5 copy-start.6
  21.9 35.2 %copy-start.5 = (bf16[8,4,4,24,256]{4,3,2,1,0:T(8,128)(2,1)}, bf16[8,4,4,24,256]{4,3,2,1,0:T(8,128)(2,1)S(1)}, u32[]{:S(2)}) copy-start(bf16[8,4,4,24,256]{4,3,2,1,0:T(8,128)(2,1)S(1)} %get-tuple-element.13) | copy-start | bytes 4718596
  86.7 1.1 copy-start.3
  87.9 29.1 %all-to-all-start.2 = ((bf16[128,24,256]{2,1,0:T(8,128)(2,1)}), bf16[128,24,256]{2,1,0:T(8,128)(2,1)S(1)}, u32[]{:S(2)}, u32[]{:S(2)}) async-start(bf16[128,24,256]{2,1,0:T(8,128)(2,1)} %bitcast.47), calls=%async_computation.2 | async-start | bytes 3145728 | tf_op jit(solution)/shard_map/all_to_all | solution.py:251
  92.6 65.4 %collective-permute-start.9 = (bf16[6,512,256]{2,1,0:T(8,128)(2,1)}, bf16[6,512,256]{2,1,0:T(8,128)(2,1)}, u32[]{:S(2)}, u32[]{:S(2)}) collective-permute-start(bf16[6,512,256]{2,1,0:T(8,128)(2,1)} %regroup.4), channel_id=1, source_target_pairs={{0,2},{2,0},{1,3},{3,1},{4,6},{6,4},{5,7},{7,5},{8,10},{10,8},{9,1... | collective-permute-start | bytes 4718600 | tf_op jit(solution)/shard_map/ppermute | solution.py:242
  93.8 64.2 %collective-permute-start.10 = (bf16[6,512,256]{2,1,0:T(8,128)(2,1)}, bf16[6,512,256]{2,1,0:T(8,128)(2,1)}, u32[]{:S(2)}, u32[]{:S(2)}) collective-permute-start(bf16[6,512,256]{2,1,0:T(8,128)(2,1)} %regroup.4), channel_id=1, source_target_pairs={{0,1},{1,0},{2,3},{3,2},{4,5},{5,4},{6,7},{7,6},{8,9},{9,8},{10,11... | collective-permute-start | bytes 4718600 | tf_op jit(solution)/shard_map/ppermute | solution.py:242
  118.2 48.8 %copy-start = (bf16[6,512,256]{2,1,0:T(8,128)(2,1)}, bf16[6,512,256]{2,1,0:T(8,128)(2,1)S(1)}, u32[]{:S(2)}) copy-start(bf16[6,512,256]{2,1,0:T(8,128)(2,1)S(1)} %regroup.6) | copy-start | bytes 4718596
  118.2 44.9 %all-to-all-start.3 = ((bf16[32,24,1024]{2,1,0:T(8,128)(2,1)}), bf16[32,24,1024]{2,1,0:T(8,128)(2,1)S(1)}, u32[]{:S(2)}, u32[]{:S(2)}) async-start(bf16[32,24,1024]{2,1,0:T(8,128)(2,1)} %bitcast.51), calls=%async_computation.3 | async-start | bytes 3145728 | tf_op jit(solution)/shard_map/all_to_all | solution.py:251
  122.2 44.7 %collective-permute-start.8 = (bf16[6,128,1024]{2,1,0:T(8,128)(2,1)}, bf16[6,128,1024]{2,1,0:T(8,128)(2,1)}, u32[]{:S(2)}, u32[]{:S(2)}) collective-permute-start(bf16[6,128,1024]{2,1,0:T(8,128)(2,1)} %copy-done.3), channel_id=1, source_target_pairs={{0,8},{4,12},{8,0},{12,4},{1,9},{5,13},{9,1},{13,5},{2,10},{6,14},... | collective-permute-start | bytes 4718600 | tf_op jit(solution)/shard_map/ppermute | solution.py:239
  124.1 68.8 %collective-permute-start.7 = (bf16[6,128,1024]{2,1,0:T(8,128)(2,1)}, bf16[6,128,1024]{2,1,0:T(8,128)(2,1)}, u32[]{:S(2)}, u32[]{:S(2)}) collective-permute-start(bf16[6,128,1024]{2,1,0:T(8,128)(2,1)} %copy-done.3), channel_id=1, source_target_pairs={{0,12},{4,0},{8,4},{12,8},{1,13},{5,1},{9,5},{13,9},{2,14},{6,2},{... | collective-permute-start | bytes 4718600 | tf_op jit(solution)/shard_map/ppermute | solution.py:239
  125.7 70.0 %collective-permute-start.6 = (bf16[6,128,1024]{2,1,0:T(8,128)(2,1)}, bf16[6,128,1024]{2,1,0:T(8,128)(2,1)}, u32[]{:S(2)}, u32[]{:S(2)}) collective-permute-start(bf16[6,128,1024]{2,1,0:T(8,128)(2,1)} %copy-done.3), channel_id=1, source_target_pairs={{0,4},{4,8},{8,12},{12,0},{1,5},{5,9},{9,13},{13,1},{2,6},{6,10},{... | collective-permute-start | bytes 4718600 | tf_op jit(solution)/shard_map/ppermute | solution.py:239
  158.0 39.2 %collective-permute-start.11 = (bf16[6,512,256]{2,1,0:T(8,128)(2,1)}, bf16[6,512,256]{2,1,0:T(8,128)(2,1)}, u32[]{:S(2)}, u32[]{:S(2)}) collective-permute-start(bf16[6,512,256]{2,1,0:T(8,128)(2,1)} %collective-permute-done.9), channel_id=1, source_target_pairs={{0,1},{1,0},{2,3},{3,2},{4,5},{5,4},{6,7},{7,6},{8,9},{9,8},{10,11... | collective-permute-start | bytes 4718600 | tf_op jit(solution)/shard_map/ppermute | solution.py:242
  158.0 39.7 %collective-permute-start.3 = (bf16[6,512,256]{2,1,0:T(8,128)(2,1)S(1)}, bf16[6,512,256]{2,1,0:T(8,128)(2,1)}, u32[]{:S(2)}, u32[]{:S(2)}) collective-permute-start(bf16[6,512,256]{2,1,0:T(8,128)(2,1)S(1)} %regroup.6), channel_id=1, source_target_pairs={{0,2},{2,0},{1,3},{3,1},{4,6},{6,4},{5,7},{7,5},{8,10},{10,8},{9,1... | collective-permute-start | bytes 4718600 | tf_op jit(solution)/shard_map/ppermute | solution.py:242
  163.1 1.1 copy-start.1
  164.3 1.4 copy-start.2
  167.0 44.8 %collective-permute-start.4 = (bf16[6,512,256]{2,1,0:T(8,128)(2,1)S(1)}, bf16[6,512,256]{2,1,0:T(8,128)(2,1)}, u32[]{:S(2)}, u32[]{:S(2)}) collective-permute-start(bf16[6,512,256]{2,1,0:T(8,128)(2,1)S(1)} %regroup.6), channel_id=1, source_target_pairs={{0,1},{1,0},{2,3},{3,2},{4,5},{5,4},{6,7},{7,6},{8,9},{9,8},{10,11... | collective-permute-start | bytes 4718600 | tf_op jit(solution)/shard_map/ppermute | solution.py:242
  192.8 39.0 %collective-permute-start.2 = (bf16[6,128,1024]{2,1,0:T(8,128)(2,1)S(1)}, bf16[6,128,1024]{2,1,0:T(8,128)(2,1)}, u32[]{:S(2)}, u32[]{:S(2)}) collective-permute-start(bf16[6,128,1024]{2,1,0:T(8,128)(2,1)S(1)} %regroup.7), channel_id=1, source_target_pairs={{0,8},{4,12},{8,0},{12,4},{1,9},{5,13},{9,1},{13,5},{2,10},{6,14},... | collective-permute-start | bytes 4718600 | tf_op jit(solution)/shard_map/ppermute | solution.py:239
  195.7 68.8 %collective-permute-start.1 = (bf16[6,128,1024]{2,1,0:T(8,128)(2,1)S(1)}, bf16[6,128,1024]{2,1,0:T(8,128)(2,1)}, u32[]{:S(2)}, u32[]{:S(2)}) collective-permute-start(bf16[6,128,1024]{2,1,0:T(8,128)(2,1)S(1)} %regroup.7), channel_id=1, source_target_pairs={{0,12},{4,0},{8,4},{12,8},{1,13},{5,1},{9,5},{13,9},{2,14},{6,2},{... | collective-permute-start | bytes 4718600 | tf_op jit(solution)/shard_map/ppermute | solution.py:239
  197.2 67.3 %collective-permute-start = (bf16[6,128,1024]{2,1,0:T(8,128)(2,1)S(1)}, bf16[6,128,1024]{2,1,0:T(8,128)(2,1)}, u32[]{:S(2)}, u32[]{:S(2)}) collective-permute-start(bf16[6,128,1024]{2,1,0:T(8,128)(2,1)S(1)} %regroup.7), channel_id=1, source_target_pairs={{0,4},{4,8},{8,12},{12,0},{1,5},{5,9},{9,13},{13,1},{2,6},{6,10},{... | collective-permute-start | bytes 4718600 | tf_op jit(solution)/shard_map/ppermute | solution.py:239
  197.7 66.7 %collective-permute-start.5 = (bf16[6,512,256]{2,1,0:T(8,128)(2,1)}, bf16[6,512,256]{2,1,0:T(8,128)(2,1)}, u32[]{:S(2)}, u32[]{:S(2)}) collective-permute-start(bf16[6,512,256]{2,1,0:T(8,128)(2,1)} %collective-permute-done.3), channel_id=1, source_target_pairs={{0,1},{1,0},{2,3},{3,2},{4,5},{5,4},{6,7},{7,6},{8,9},{9,8},{10,11... | collective-permute-start | bytes 4718600 | tf_op jit(solution)/shard_map/ppermute | solution.py:242
  197.8 1.4 copy-start.4

commit v2 on v1

--- a/solution.py
+++ b/solution.py
@@ -12,7 +12,7 @@
 CHAN_COL = ("chan", "col_0", "col_1")
 CHAN_ROW_COL = ("chan", "row", "col_0", "col_1")
 CHUNKS = 2
-STEPS = (("row", (0,)), ("col", (0,)), ("row", (1,)), ("col", (1,)))
+STEPS = (("col", (0,)), ("row", (0, 1)), ("col", (1,)))
 F32 = jnp.float32
 BF16 = jnp.bfloat16
 
@@ -65,7 +65,7 @@
         part_ref[pl.ds(to + depth, group)] = lo
         return 0
 
-    lax.fori_loop(0, slots * 2 * steps, filter_rows, 0, unroll=4)
+    lax.fori_loop(0, slots * 2 * steps, filter_rows, 0, unroll=32)
     out = jnp.dot(hi_ref[...], part_ref[0:depth], preferred_element_type=F32)
     out = out + jnp.dot(hi_ref[...], part_ref[depth:], preferred_element_type=F32)
     out = out + jnp.dot(lo_ref[...], part_ref[0:depth], preferred_element_type=F32)
@@ -160,13 +160,16 @@
 
 
 def correlate_kernel(order_ref, *refs):
-    cols, pieces = refs[0:4], refs[4:8]
+    cols, pieces = refs[0:5], refs[5:9]
     out_ref, a_ref, b_ref = refs[-3:]
     frames = cols[0].shape[4]
     quarter = pieces[0].shape[3]
+    half = cols[3].shape[2]
+    places = (slice(None), slice(None), slice(None), slice(0, half), slice(half, None))
     for plane in range(2):
-        for k, ref in enumerate(cols):
-            b_ref[:, order_ref[k], :, plane * frames : (plane + 1) * frames] = ref[0, plane]
+        for k, (ref, place) in enumerate(zip(cols, places)):
+            to = slice(plane * frames, (plane + 1) * frames)
+            b_ref[place, order_ref[min(k, 3)], :, to] = ref[0, plane]
         for k, ref in enumerate(pieces):
             at = pl.multiple_of(order_ref[4 + k] * quarter, quarter)
             part = ref[0, plane]
@@ -183,19 +186,19 @@
         )
 
 
-def correlate(order, cols, pieces, out, chunk, total):
+def correlate(order, cols, pieces, out, first, total):
     channels, _, size, quarter = pieces[0].shape
     _, _, chans, rows_of, frames = cols[0].shape
-    col_spec = pl.BlockSpec((1, 2, chans, rows_of, frames), lambda k, s: (k, 0, 0, 0, 0))
     row_spec = pl.BlockSpec((1, 2, size, quarter), lambda k, s: (k, 0, 0, 0))
-    in_specs = [col_spec] * 4 + [row_spec] * 4
+    in_specs = [
+        pl.BlockSpec((1, *c.shape[1:]), lambda k, s: (k, 0, 0, 0, 0)) for c in cols
+    ] + [row_spec] * 4
     operands = [order, *cols, *pieces]
     aliases = {}
     if out is not None:
         in_specs.append(pl.BlockSpec(memory_space=pl.ANY))
         aliases = {len(operands): 0}
         operands.append(out)
-    first = chunk * channels
     return pl.pallas_call(
         correlate_kernel,
         grid_spec=pltpu.PrefetchScalarGridSpec(
@@ -241,28 +244,34 @@
     def swap(x, axis):
         return lax.ppermute(x, axis, [(0, 1), (1, 0)])
 
-    cols, rows = [None] * CHUNKS, [None] * CHUNKS
-    token = None
-    for (kind, pieces), block in zip(STEPS, sent):
-        axes = CHAN_COL if kind == "col" else CHAN_ROW_COL
+    def after(x, *others):
+        return lax.optimization_barrier((x, others))[0]
+
+    def exchange(block, axes):
         block = block.reshape(-1, *block.shape[-2:])
-        if token is not None:
-            block, token = lax.optimization_barrier((block, token))
         block = lax.all_to_all(block, axes, split_axis=0, concat_axis=0, tiled=True)
-        block = regroup(block, kinds, slots)
-        token = block[0]
-        for piece, part in zip(pieces, block):
-            if kind == "col":
-                parts = [part, turn(part, 1), turn(part, -1), turn(part, 2)]
-                parts = [c.reshape(kinds // 2, 2, chan_count, -1, c.shape[2]) for c in parts]
-                cols[piece] = parts
-            else:
-                parts = [part, swap(part, "col_0")]
-                parts += [swap(r, "col_1") for r in parts]
-                rows[piece] = [r.reshape(kinds // 2, 2, *r.shape[1:]) for r in parts]
+        return regroup(block, kinds, slots)
+
+    def onward(up, down):
+        half = up.shape[1] // 2
+        return turn(up[:, :half], 1), turn(down[:, half:], -1)
+
+    (first,) = exchange(sent[0], CHAN_COL)
+    near_0 = turn(first, 1), turn(first, -1)
+    rows = exchange(after(sent[1], first), CHAN_ROW_COL)
+    rows = [(r, swap(r, "col_0")) for r in rows]
+    (second,) = exchange(after(sent[2], *rows[0], *near_0), CHAN_COL)
+    far_0 = onward(*near_0)
+    second = after(second, *far_0)
+    near_1 = turn(second, 1), turn(second, -1)
+    cols = [(first, *near_0, *far_0), (second, *near_1, *onward(*near_1))]
+    rows[1] = tuple(after(r, *near_1) for r in rows[1])
+    rows = [(*r, *(swap(q, "col_1") for q in r)) for r in rows]
+    cols = [[c.reshape(kinds // 2, 2, -1, 16, c.shape[2]) for c in p] for p in cols]
+    rows = [[r.reshape(kinds // 2, 2, *r.shape[1:]) for r in p] for p in rows]
     out = None
     for chunk in range(CHUNKS):
-        out = correlate(order, cols[chunk], rows[chunk], out, chunk, per_chan)
+        out = correlate(order, cols[chunk], rows[chunk], out, chunk * (kinds // 2), per_chan)
     return out
 
 

time: 278 us -> 245 us (0.88)
  blocking collectives: 61.4 us -> 30.4 us
  waiting for transfers between devices: 137 us -> 131 us
  local copies, waits for them, and re-layouts: 6.19 us -> 10.1 us
  starting transfers between devices: 20.2 us -> 23.7 us
    ppermute x6 -> x8, waiting for transfers between devices: 78.3 us -> 40.4 us  [turn(): lax.ppermute(x, 'row', [(k, (k + by) % row_count) for k in range(row_coun...]
    all_to_all x2 -> x1, blocking collectives: 61.4 us -> 30.4 us  [exchange(): block = lax.all_to_all(block, axes, split_axis=0, concat_axis=0, tiled=True)]
    all_to_all x2, waiting for transfers between devices: 26.9 us -> 54.8 us  [exchange(): block = lax.all_to_all(block, axes, split_axis=0, concat_axis=0, tiled=True)]
    slice x0 -> x4, local copies, waits for them, and re-layouts: none -> 5.21 us  [onward(): return (turn(up[:, :half], 1), turn(down[:, half:], -1))]
    ppermute x6, waiting for transfers between devices: 31.9 us -> 35.8 us  [swap(): return lax.ppermute(x, axis, [(0, 1), (1, 0)])]
    pallas_call x1, Pallas kernels: 20.3 us -> 17.2 us  [spectra(): pl.pallas_call(spectra_kernel, grid=(panels,), in_specs=[pl.BlockSpec((2,...]
    all_to_all x2, starting transfers between devices: 8.78 us -> 11.6 us  [exchange(): block = lax.all_to_all(block, axes, split_axis=0, concat_axis=0, tiled=True)]
    pallas_call x4 -> x3, Pallas kernels: 5.89 us -> 6.96 us  [regroup(): pl.pallas_call(functools.partial(regroup_kernel, size, slots), grid=(step...]
  transfers between devices with their start and end apart: 14 -> 16, of which waited for: 6 -> 10; matrix products, arithmetic and copies ran while one was open for 0% -> 2% of each run, Pallas kernels for 5% -> 7%
where the time goes in v2:
time: 245 us
  waiting for transfers between devices  131 us (53%)
  Pallas kernels  49.1 us (20%)
  blocking collectives  30.4 us (12%)
  starting transfers between devices  23.7 us (10%)
  local copies, waits for them, and re-layouts  10.1 us (4%)
    all_to_all x2, waiting for transfers between devices, exchange(): block = lax.all_to_all(block, axes, split_axis=0, concat_axis=0, tiled=True)  54.8 us
    ppermute x8, waiting for transfers between devices, turn(): lax.ppermute(x, 'row', [(k, (k + by) % row_count) for k in range(row_coun...  40.4 us
    ppermute x6, waiting for transfers between devices, swap(): return lax.ppermute(x, axis, [(0, 1), (1, 0)])  35.8 us
    all_to_all x1, blocking collectives, exchange(): block = lax.all_to_all(block, axes, split_axis=0, concat_axis=0, tiled=True)  30.4 us
    pallas_call x2, Pallas kernels, correlate(): pl.pallas_call(correlate_kernel, grid_spec=pltpu.PrefetchScalarGridSpec(n...  24.9 us
    pallas_call x1, Pallas kernels, spectra(): pl.pallas_call(spectra_kernel, grid=(panels,), in_specs=[pl.BlockSpec((2,...  17.2 us
    all_to_all x2, starting transfers between devices, exchange(): block = lax.all_to_all(block, axes, split_axis=0, concat_axis=0, tiled=True)  11.6 us
    ppermute x8, starting transfers between devices, turn(): lax.ppermute(x, 'row', [(k, (k + by) % row_count) for k in range(row_coun...  8.31 us
  transfers between devices with their start and end apart: 16, of which 10 were waited for; matrix products, arithmetic and copies ran while one was open for 2% of the time, Pallas kernels for 7%

profile of v2, /device:TPU:0, one launch (start us, length us, event | category | flops | bytes accessed | tf_op | source)
XLA Modules:
  0.0 245.0 jit_solution(6811203587243377144)
XLA Ops:
  1.6 17.2 %spectra.1 = (bf16[8,4,24,1024]{3,2,1,0:T(8,128)(2,1)S(1)}, bf16[8,4,4,48,256]{4,3,2,1,0:T(8,128)(2,1)}, bf16[8,4,24,1024]{3,2,1,0:T(8,128)(2,1)S(1)}) custom-call(bf16[2,4,4,64,1031]{4,3,2,1,0:T(8,128)(2,1)} %volt_ref.1, f32[8,64,128]{2,1,0:T(8,128)S(1)} %broadcast_in_dim.2.win_ref, bf16[384,512]{1,0:T(8,128)(2,1)S(1)} %get-tuple-element.26.hi_ref, ...), custom_call_target="tpu_custom_call" | custom-call | tf_op jit(solution)/shard_map/spectra/pallas_call | solution.py:104
  20.1 30.4 %all_to_all.15 = bf16[32,24,1024]{2,1,0:T(8,128)(2,1)S(1)} all-to-all(bf16[32,24,1024]{2,1,0:T(8,128)(2,1)S(1)} %bitcast.47), channel_id=1, replica_groups=mesh['chan'=8,'row'=4,'col_0'=2,'col_1'=2] {'chan','col_0','col_1'}, dimensions={0} | all-to-all | bytes 3145728 | tf_op jit(solution)/shard_map/all_to_all | solution.py:252
  50.5 1.3 regroup.3
  51.8 7.5 %all-to-all-start.1 = ((bf16[128,48,256]{2,1,0:T(8,128)(2,1)}), bf16[128,48,256]{2,1,0:T(8,128)(2,1)}, u32[]{:S(2)}, u32[]{:S(2)}) async-start(bf16[128,48,256]{2,1,0:T(8,128)(2,1)} %bitcast.50), calls=%async_computation.1 | async-start | bytes 6291456 | tf_op jit(solution)/shard_map/all_to_all | solution.py:252
  59.2 2.2 collective-permute-start.2
  61.5 38.7 %all-to-all-done.1 = bf16[128,48,256]{2,1,0:T(8,128)(2,1)} async-done(((bf16[128,48,256]{2,1,0:T(8,128)(2,1)}), bf16[128,48,256]{2,1,0:T(8,128)(2,1)}, u32[]{:S(2)}, u32[]{:S(2)}) %all-to-all-start.1) | async-done | bytes 3145760 | tf_op jit(solution)/shard_map/all_to_all | solution.py:252
  100.1 4.4 %regroup.4 = (bf16[6,512,256]{2,1,0:T(8,128)(2,1)S(1)}, bf16[6,512,256]{2,1,0:T(8,128)(2,1)}) custom-call(bf16[6144,256]{1,0:T(8,128)(2,1)} %bitcast.13.x_ref), custom_call_target="tpu_custom_call" | custom-call | flops 1207959552 | bytes 6291456 | tf_op jit(solution)/shard_map/regroup/pallas_call | solution.py:146
  105.5 24.5 %collective-permute-done.2 = bf16[6,128,1024]{2,1,0:T(8,128)(2,1)} collective-permute-done((bf16[6,128,1024]{2,1,0:T(8,128)(2,1)S(1)}, bf16[6,128,1024]{2,1,0:T(8,128)(2,1)}, u32[]{:S(2)}, u32[]{:S(2)}) %collective-permute-start.2) | collective-permute-done | bytes 1572896 | tf_op jit(solution)/shard_map/ppermute | solution.py:242
  130.0 10.4 %collective-permute-done = bf16[6,512,256]{2,1,0:T(8,128)(2,1)} collective-permute-done((bf16[6,512,256]{2,1,0:T(8,128)(2,1)S(1)}, bf16[6,512,256]{2,1,0:T(8,128)(2,1)}, u32[]{:S(2)}, u32[]{:S(2)}) %collective-permute-start) | collective-permute-done | bytes 1572896 | tf_op jit(solution)/shard_map/ppermute | solution.py:245
  140.4 4.2 %all-to-all-start.2 = ((bf16[32,24,1024]{2,1,0:T(8,128)(2,1)}), bf16[32,24,1024]{2,1,0:T(8,128)(2,1)S(1)}, u32[]{:S(2)}, u32[]{:S(2)}) async-start(bf16[32,24,1024]{2,1,0:T(8,128)(2,1)} %bitcast.46), calls=%async_computation.2 | async-start | bytes 3145728 | tf_op jit(solution)/shard_map/all_to_all | solution.py:252
  144.6 2.2 slice.17
  146.9 1.5 collective-permute-start.4
  149.9 1.8 collective-permute-start.9
  151.7 16.1 %all-to-all-done.2 = bf16[32,24,1024]{2,1,0:T(8,128)(2,1)S(1)} async-done(((bf16[32,24,1024]{2,1,0:T(8,128)(2,1)}), bf16[32,24,1024]{2,1,0:T(8,128)(2,1)S(1)}, u32[]{:S(2)}, u32[]{:S(2)}) %all-to-all-start.2) | async-done | bytes 1572896 | tf_op jit(solution)/shard_map/all_to_all | solution.py:252
  167.8 1.3 regroup.5
  170.7 1.7 collective-permute-start.5
  172.9 25.3 %collective-permute-done.9 = bf16[6,512,256]{2,1,0:T(8,128)(2,1)} collective-permute-done((bf16[6,512,256]{2,1,0:T(8,128)(2,1)}, bf16[6,512,256]{2,1,0:T(8,128)(2,1)}, u32[]{:S(2)}, u32[]{:S(2)}) %collective-permute-start.9) | collective-permute-done | bytes 1572896 | tf_op jit(solution)/shard_map/ppermute | solution.py:245
  198.2 7.6 %collective-permute-done.6 = bf16[6,128,1024]{2,1,0:T(8,128)(2,1)S(1)} collective-permute-done((bf16[6,128,1024]{2,1,0:T(8,128)(2,1)S(1)}, bf16[6,128,1024]{2,1,0:T(8,128)(2,1)S(1)}, u32[]{:S(2)}, u32[]{:S(2)}) %collective-permute-start.6) | collective-permute-done | bytes 1572896 | tf_op jit(solution)/shard_map/ppermute | solution.py:242
  205.8 1.9 collective-permute-done.5
  213.5 1.4 copy-done.6
  214.9 12.4 %correlate.2.refs_9_ = f32[6,2,512,512]{3,2,1,0:T(8,128)} custom-call(s32[8]{0:T(128)S(1)} %stack.40.order_ref, bf16[3,2,8,16,1024]{4,3,2,1,0:T(8,128)(2,1)S(1)} %bitcast.43, bf16[3,2,8,16,1024]{4,3,2,1,0:T(8,128)(2,1)S(1)} %bitcast.45, bf16[3,2,8,16,1024]{4,3,2,1,0:T(8,128)(2,1)} %bitcast.27.refs_2_, bf16[3,2,4,16,1024]{4,3,2,1,0:T(8,128)(2,1)} %bitcast.28.refs_3_, ...), custom_call_target="tpu_custom_call" | custom-call | flops 6442450944 | bytes 18874368 | tf_op jit(solution)/shard_map/correlate/pallas_call | solution.py:202
  227.4 1.6 collective-permute-done.8
  229.0 3.6 %collective-permute-done.7 = bf16[6,64,1024]{2,1,0:T(8,128)(2,1)} collective-permute-done((bf16[6,64,1024]{2,1,0:T(8,128)(2,1)}, bf16[6,64,1024]{2,1,0:T(8,128)(2,1)}, u32[]{:S(2)}, u32[]{:S(2)}) %collective-permute-start.7) | collective-permute-done | bytes 786464 | tf_op jit(solution)/shard_map/ppermute | solution.py:242
  232.6 12.5 %correlate.3 = f32[6,2,512,512]{3,2,1,0:T(8,128)} custom-call(s32[8]{0:T(128)S(1)} %stack.40.order_ref, bf16[3,2,8,16,1024]{4,3,2,1,0:T(8,128)(2,1)S(1)} %bitcast.40, bf16[3,2,8,16,1024]{4,3,2,1,0:T(8,128)(2,1)S(1)} %bitcast.44, bf16[3,2,8,16,1024]{4,3,2,1,0:T(8,128)(2,1)} %bitcast.49, ...), custom_call_target="tpu_custom_call", output_to_operand_aliasing={{}: (10, {})} | custom-call | flops 6442450944 | bytes 18874368 | tf_op jit(solution)/shard_map/correlate/pallas_call | solution.py:202
  (55 shorter events, 13.1 us)
Async XLA Ops:
  51.8 9.7 %copy-start = (bf16[6,128,1024]{2,1,0:T(8,128)(2,1)}, bf16[6,128,1024]{2,1,0:T(8,128)(2,1)S(1)}, u32[]{:S(2)}) copy-start(bf16[6,128,1024]{2,1,0:T(8,128)(2,1)S(1)} %regroup.3) | copy-start | bytes 4718596
  51.8 48.4 %all-to-all-start.1 = ((bf16[128,48,256]{2,1,0:T(8,128)(2,1)}), bf16[128,48,256]{2,1,0:T(8,128)(2,1)}, u32[]{:S(2)}, u32[]{:S(2)}) async-start(bf16[128,48,256]{2,1,0:T(8,128)(2,1)} %bitcast.50), calls=%async_computation.1 | async-start | bytes 6291456 | tf_op jit(solution)/shard_map/all_to_all | solution.py:252
  59.2 70.7 %collective-permute-start.2 = (bf16[6,128,1024]{2,1,0:T(8,128)(2,1)S(1)}, bf16[6,128,1024]{2,1,0:T(8,128)(2,1)}, u32[]{:S(2)}, u32[]{:S(2)}) collective-permute-start(bf16[6,128,1024]{2,1,0:T(8,128)(2,1)S(1)} %regroup.3), channel_id=1, source_target_pairs={{0,12},{4,0},{8,4},{12,8},{1,13},{5,1},{9,5},{13,9},{2,14},{6,2},{... | collective-permute-start | bytes 4718600 | tf_op jit(solution)/shard_map/ppermute | solution.py:242
  61.5 68.5 %collective-permute-start.1 = (bf16[6,128,1024]{2,1,0:T(8,128)(2,1)S(1)}, bf16[6,128,1024]{2,1,0:T(8,128)(2,1)S(1)}, u32[]{:S(2)}, u32[]{:S(2)}) collective-permute-start(bf16[6,128,1024]{2,1,0:T(8,128)(2,1)S(1)} %regroup.3), channel_id=1, source_target_pairs={{0,4},{4,8},{8,12},{12,0},{1,5},{5,9},{9,13},{13,1},{2,6},{6,10},{... | collective-permute-start | bytes 4718600 | tf_op jit(solution)/shard_map/ppermute | solution.py:242
  104.5 25.4 %copy-start.8 = (bf16[6,512,256]{2,1,0:T(8,128)(2,1)}, bf16[6,512,256]{2,1,0:T(8,128)(2,1)S(1)}, u32[]{:S(2)}) copy-start(bf16[6,512,256]{2,1,0:T(8,128)(2,1)S(1)} %get-tuple-element.19) | copy-start | bytes 4718596
  104.5 35.9 %collective-permute-start = (bf16[6,512,256]{2,1,0:T(8,128)(2,1)S(1)}, bf16[6,512,256]{2,1,0:T(8,128)(2,1)}, u32[]{:S(2)}, u32[]{:S(2)}) collective-permute-start(bf16[6,512,256]{2,1,0:T(8,128)(2,1)S(1)} %get-tuple-element.19), channel_id=1, source_target_pairs={{0,2},{2,0},{1,3},{3,1},{4,6},{6,4},{5,7},{7,5},{8,10},{10,8},{9,1... | collective-permute-start | bytes 4718600 | tf_op jit(solution)/shard_map/ppermute | solution.py:245
  130.0 10.5 %copy-start.4 = (bf16[6,128,1024]{2,1,0:T(8,128)(2,1)}, bf16[6,128,1024]{2,1,0:T(8,128)(2,1)S(1)}, u32[]{:S(2)}) copy-start(bf16[6,128,1024]{2,1,0:T(8,128)(2,1)S(1)} %collective-permute-done.1) | copy-start | bytes 4718596
  140.4 27.3 %all-to-all-start.2 = ((bf16[32,24,1024]{2,1,0:T(8,128)(2,1)}), bf16[32,24,1024]{2,1,0:T(8,128)(2,1)S(1)}, u32[]{:S(2)}, u32[]{:S(2)}) async-start(bf16[32,24,1024]{2,1,0:T(8,128)(2,1)} %bitcast.46), calls=%async_computation.2 | async-start | bytes 3145728 | tf_op jit(solution)/shard_map/all_to_all | solution.py:252
  144.6 3.8 %copy-start.5 = (bf16[6,128,1024]{2,1,0:T(8,128)(2,1)S(1)}, bf16[6,128,1024]{2,1,0:T(8,128)(2,1)}, u32[]{:S(2)}) copy-start(bf16[6,128,1024]{2,1,0:T(8,128)(2,1)} %copy-done.4) | copy-start | bytes 4718596
  146.9 22.2 %collective-permute-start.4 = (bf16[6,64,1024]{2,1,0:T(8,128)(2,1)}, bf16[6,64,1024]{2,1,0:T(8,128)(2,1)}, u32[]{:S(2)}, u32[]{:S(2)}) collective-permute-start(bf16[6,64,1024]{2,1,0:T(8,128)(2,1)} %slice.17), channel_id=1, source_target_pairs={{0,12},{4,0},{8,4},{12,8},{1,13},{5,1},{9,5},{13,9},{2,14},{6,2},{... | collective-permute-start | bytes 2359304 | tf_op jit(solution)/shard_map/ppermute | solution.py:242
  149.4 21.0 %collective-permute-start.3 = (bf16[6,64,1024]{2,1,0:T(8,128)(2,1)}, bf16[6,64,1024]{2,1,0:T(8,128)(2,1)}, u32[]{:S(2)}, u32[]{:S(2)}) collective-permute-start(bf16[6,64,1024]{2,1,0:T(8,128)(2,1)} %slice.16), channel_id=1, source_target_pairs={{0,4},{4,8},{8,12},{12,0},{1,5},{5,9},{9,13},{13,1},{2,6},{6,10},{... | collective-permute-start | bytes 2359304 | tf_op jit(solution)/shard_map/ppermute | solution.py:242
  149.9 48.3 %collective-permute-start.9 = (bf16[6,512,256]{2,1,0:T(8,128)(2,1)}, bf16[6,512,256]{2,1,0:T(8,128)(2,1)}, u32[]{:S(2)}, u32[]{:S(2)}) collective-permute-start(bf16[6,512,256]{2,1,0:T(8,128)(2,1)} %get-tuple-element.23), channel_id=1, source_target_pairs={{0,2},{2,0},{1,3},{3,1},{4,6},{6,4},{5,7},{7,5},{8,10},{10,8},{9,1... | collective-permute-start | bytes 4718600 | tf_op jit(solution)/shard_map/ppermute | solution.py:245
  167.8 4.6 %copy-start.9 = (bf16[6,512,256]{2,1,0:T(8,128)(2,1)S(1)}, bf16[6,512,256]{2,1,0:T(8,128)(2,1)}, u32[]{:S(2)}) copy-start(bf16[6,512,256]{2,1,0:T(8,128)(2,1)} %copy-done.8) | copy-start | bytes 4718596
  169.1 44.5 %copy-start.1 = (bf16[6,128,1024]{2,1,0:T(8,128)(2,1)S(1)}, bf16[6,128,1024]{2,1,0:T(8,128)(2,1)}, u32[]{:S(2)}) copy-start(bf16[6,128,1024]{2,1,0:T(8,128)(2,1)} %copy-done) | copy-start | bytes 4718596
  170.3 35.4 %collective-permute-start.6 = (bf16[6,128,1024]{2,1,0:T(8,128)(2,1)S(1)}, bf16[6,128,1024]{2,1,0:T(8,128)(2,1)S(1)}, u32[]{:S(2)}, u32[]{:S(2)}) collective-permute-start(bf16[6,128,1024]{2,1,0:T(8,128)(2,1)S(1)} %regroup.5), channel_id=1, source_target_pairs={{0,12},{4,0},{8,4},{12,8},{1,13},{5,1},{9,5},{13,9},{2,14},{6,2},{... | collective-permute-start | bytes 4718600 | tf_op jit(solution)/shard_map/ppermute | solution.py:242
  170.7 37.0 %collective-permute-start.5 = (bf16[6,128,1024]{2,1,0:T(8,128)(2,1)S(1)}, bf16[6,128,1024]{2,1,0:T(8,128)(2,1)S(1)}, u32[]{:S(2)}, u32[]{:S(2)}) collective-permute-start(bf16[6,128,1024]{2,1,0:T(8,128)(2,1)S(1)} %regroup.5), channel_id=1, source_target_pairs={{0,4},{4,8},{8,12},{12,0},{1,5},{5,9},{9,13},{13,1},{2,6},{6,10},{... | collective-permute-start | bytes 4718600 | tf_op jit(solution)/shard_map/ppermute | solution.py:242
  172.4 38.7 %collective-permute-start.12 = (bf16[6,512,256]{2,1,0:T(8,128)(2,1)S(1)}, bf16[6,512,256]{2,1,0:T(8,128)(2,1)S(1)}, u32[]{:S(2)}, u32[]{:S(2)}) collective-permute-start(bf16[6,512,256]{2,1,0:T(8,128)(2,1)S(1)} %copy-done.9), channel_id=1, source_target_pairs={{0,1},{1,0},{2,3},{3,2},{4,5},{5,4},{6,7},{7,6},{8,9},{9,8},{10,11... | collective-permute-start | bytes 4718600 | tf_op jit(solution)/shard_map/ppermute | solution.py:245
  172.4 41.2 %collective-permute-start.13 = (bf16[6,512,256]{2,1,0:T(8,128)(2,1)}, bf16[6,512,256]{2,1,0:T(8,128)(2,1)}, u32[]{:S(2)}, u32[]{:S(2)}) collective-permute-start(bf16[6,512,256]{2,1,0:T(8,128)(2,1)} %collective-permute-done), channel_id=1, source_target_pairs={{0,1},{1,0},{2,3},{3,2},{4,5},{5,4},{6,7},{7,6},{8,9},{9,8},{10,11... | collective-permute-start | bytes 4718600 | tf_op jit(solution)/shard_map/ppermute | solution.py:245
  205.8 5.3 %copy-start.10 = (bf16[6,128,1024]{2,1,0:T(8,128)(2,1)}, bf16[6,128,1024]{2,1,0:T(8,128)(2,1)S(1)}, u32[]{:S(2)}) copy-start(bf16[6,128,1024]{2,1,0:T(8,128)(2,1)S(1)} %collective-permute-done.6) | copy-start | bytes 4718596
  207.7 24.8 %collective-permute-start.10 = (bf16[6,512,256]{2,1,0:T(8,128)(2,1)}, bf16[6,512,256]{2,1,0:T(8,128)(2,1)}, u32[]{:S(2)}, u32[]{:S(2)}) collective-permute-start(bf16[6,512,256]{2,1,0:T(8,128)(2,1)} %get-tuple-element.23), channel_id=1, source_target_pairs={{0,1},{1,0},{2,3},{3,2},{4,5},{5,4},{6,7},{7,6},{8,9},{9,8},{10,11... | collective-permute-start | bytes 4718600 | tf_op jit(solution)/shard_map/ppermute | solution.py:245
  207.7 24.8 %collective-permute-start.11 = (bf16[6,512,256]{2,1,0:T(8,128)(2,1)}, bf16[6,512,256]{2,1,0:T(8,128)(2,1)}, u32[]{:S(2)}, u32[]{:S(2)}) collective-permute-start(bf16[6,512,256]{2,1,0:T(8,128)(2,1)} %collective-permute-done.9), channel_id=1, source_target_pairs={{0,1},{1,0},{2,3},{3,2},{4,5},{5,4},{6,7},{7,6},{8,9},{9,8},{10,11... | collective-permute-start | bytes 4718600 | tf_op jit(solution)/shard_map/ppermute | solution.py:245
  209.2 19.8 %collective-permute-start.8 = (bf16[6,64,1024]{2,1,0:T(8,128)(2,1)}, bf16[6,64,1024]{2,1,0:T(8,128)(2,1)}, u32[]{:S(2)}, u32[]{:S(2)}) collective-permute-start(bf16[6,64,1024]{2,1,0:T(8,128)(2,1)} %slice.19), channel_id=1, source_target_pairs={{0,12},{4,0},{8,4},{12,8},{1,13},{5,1},{9,5},{13,9},{2,14},{6,2},{... | collective-permute-start | bytes 2359304 | tf_op jit(solution)/shard_map/ppermute | solution.py:242
  212.2 20.3 %collective-permute-start.7 = (bf16[6,64,1024]{2,1,0:T(8,128)(2,1)}, bf16[6,64,1024]{2,1,0:T(8,128)(2,1)}, u32[]{:S(2)}, u32[]{:S(2)}) collective-permute-start(bf16[6,64,1024]{2,1,0:T(8,128)(2,1)} %slice.18), channel_id=1, source_target_pairs={{0,4},{4,8},{8,12},{12,0},{1,5},{5,9},{9,13},{13,1},{2,6},{6,10},{... | collective-permute-start | bytes 2359304 | tf_op jit(solution)/shard_map/ppermute | solution.py:242
  214.9 17.6 %copy-start.3 = (bf16[6,128,1024]{2,1,0:T(8,128)(2,1)S(1)}, bf16[6,128,1024]{2,1,0:T(8,128)(2,1)}, u32[]{:S(2)}) copy-start(bf16[6,128,1024]{2,1,0:T(8,128)(2,1)} %copy-done.2) | copy-start | bytes 4718596
  (5 other events, 8.6 us)

commit v3 on v2

--- a/solution.py
+++ b/solution.py
@@ -247,9 +247,11 @@
     def after(x, *others):
         return lax.optimization_barrier((x, others))[0]
 
-    def exchange(block, axes):
+    def exchange(block, axes, *others):
         block = block.reshape(-1, *block.shape[-2:])
         block = lax.all_to_all(block, axes, split_axis=0, concat_axis=0, tiled=True)
+        if others:
+            block = after(block, *others)
         return regroup(block, kinds, slots)
 
     def onward(up, down):
@@ -260,11 +262,12 @@
     near_0 = turn(first, 1), turn(first, -1)
     rows = exchange(after(sent[1], first), CHAN_ROW_COL)
     rows = [(r, swap(r, "col_0")) for r in rows]
-    (second,) = exchange(after(sent[2], *rows[0], *near_0), CHAN_COL)
+    (second,) = exchange(after(sent[2], rows[0][0]), CHAN_COL, *near_0, rows[0][1])
     far_0 = onward(*near_0)
-    second = after(second, *far_0)
-    near_1 = turn(second, 1), turn(second, -1)
-    cols = [(first, *near_0, *far_0), (second, *near_1, *onward(*near_1))]
+    near_1 = after(second, *far_0)
+    near_1 = turn(near_1, 1), turn(near_1, -1)
+    far_1 = onward(*near_1)
+    cols = [(first, *near_0, *far_0), (second, *near_1, *far_1)]
     rows[1] = tuple(after(r, *near_1) for r in rows[1])
     rows = [(*r, *(swap(q, "col_1") for q in r)) for r in rows]
     cols = [[c.reshape(kinds // 2, 2, -1, 16, c.shape[2]) for c in p] for p in cols]

time: 245 us -> 236 us (0.963)
  waiting for transfers between devices: 131 us -> 123 us
    ppermute x8, waiting for transfers between devices: 40.4 us -> 33.2 us  [turn(): lax.ppermute(x, 'row', [(k, (k + by) % row_count) for k in range(row_coun...]
    ppermute x6, waiting for transfers between devices: 35.8 us -> 29.6 us  [swap(): return lax.ppermute(x, axis, [(0, 1), (1, 0)])]
    all_to_all x2, waiting for transfers between devices: 54.8 us -> 59.8 us  [exchange(): block = lax.all_to_all(block, axes, split_axis=0, concat_axis=0, tiled=True)]
  transfers between devices with their start and end apart: 16 -> 16, of which waited for: 10 -> 8; matrix products, arithmetic and copies ran while one was open for 2% -> 3% of each run, Pallas kernels for 7% -> 8%
where the time goes in v3:
time: 236 us
  waiting for transfers between devices  123 us (52%)
  Pallas kernels  49.5 us (21%)
  blocking collectives  30.4 us (13%)
  starting transfers between devices  22.6 us (10%)
  local copies, waits for them, and re-layouts  9.65 us (4%)
    all_to_all x2, waiting for transfers between devices, exchange(): block = lax.all_to_all(block, axes, split_axis=0, concat_axis=0, tiled=True)  59.8 us
    ppermute x8, waiting for transfers between devices, turn(): lax.ppermute(x, 'row', [(k, (k + by) % row_count) for k in range(row_coun...  33.2 us
    all_to_all x1, blocking collectives, exchange(): block = lax.all_to_all(block, axes, split_axis=0, concat_axis=0, tiled=True)  30.4 us
    ppermute x6, waiting for transfers between devices, swap(): return lax.ppermute(x, axis, [(0, 1), (1, 0)])  29.6 us
    pallas_call x2, Pallas kernels, correlate(): pl.pallas_call(correlate_kernel, grid_spec=pltpu.PrefetchScalarGridSpec(n...  25.1 us
    pallas_call x1, Pallas kernels, spectra(): pl.pallas_call(spectra_kernel, grid=(panels,), in_specs=[pl.BlockSpec((2,...  17.2 us
    all_to_all x2, starting transfers between devices, exchange(): block = lax.all_to_all(block, axes, split_axis=0, concat_axis=0, tiled=True)  11.8 us
    ppermute x8, starting transfers between devices, turn(): lax.ppermute(x, 'row', [(k, (k + by) % row_count) for k in range(row_coun...  8.38 us
  transfers between devices with their start and end apart: 16, of which 8 were waited for; matrix products, arithmetic and copies ran while one was open for 3% of the time, Pallas kernels for 8%

profile of v3, /device:TPU:0, one launch (start us, length us, event | category | flops | bytes accessed | tf_op | source)
XLA Modules:
  0.0 235.6 jit_solution(6525634231410676367)
XLA Ops:
  1.6 17.2 %spectra.1 = (bf16[8,4,24,1024]{3,2,1,0:T(8,128)(2,1)S(1)}, bf16[8,4,4,48,256]{4,3,2,1,0:T(8,128)(2,1)}, bf16[8,4,24,1024]{3,2,1,0:T(8,128)(2,1)S(1)}) custom-call(bf16[2,4,4,64,1031]{4,3,2,1,0:T(8,128)(2,1)} %volt_ref.1, f32[8,64,128]{2,1,0:T(8,128)S(1)} %broadcast_in_dim.2.win_ref, bf16[384,512]{1,0:T(8,128)(2,1)S(1)} %get-tuple-element.28.hi_ref, ...), custom_call_target="tpu_custom_call" | custom-call | tf_op jit(solution)/shard_map/spectra/pallas_call | solution.py:104
  18.9 1.2 copy-done.4
  20.0 30.4 %all_to_all.15 = bf16[32,24,1024]{2,1,0:T(8,128)(2,1)S(1)} all-to-all(bf16[32,24,1024]{2,1,0:T(8,128)(2,1)S(1)} %bitcast.46), channel_id=1, replica_groups=mesh['chan'=8,'row'=4,'col_0'=2,'col_1'=2] {'chan','col_0','col_1'}, dimensions={0} | all-to-all | bytes 3145728 | tf_op jit(solution)/shard_map/all_to_all | solution.py:252
  50.5 1.3 regroup.3
  51.8 7.5 %all-to-all-start.1 = ((bf16[128,48,256]{2,1,0:T(8,128)(2,1)}), bf16[128,48,256]{2,1,0:T(8,128)(2,1)}, u32[]{:S(2)}, u32[]{:S(2)}) async-start(bf16[128,48,256]{2,1,0:T(8,128)(2,1)} %bitcast.48), calls=%async_computation.1 | async-start | bytes 6291456 | tf_op jit(solution)/shard_map/all_to_all | solution.py:252
  59.2 2.2 collective-permute-start.1
  61.5 38.7 %all-to-all-done.1 = bf16[128,48,256]{2,1,0:T(8,128)(2,1)} async-done(((bf16[128,48,256]{2,1,0:T(8,128)(2,1)}), bf16[128,48,256]{2,1,0:T(8,128)(2,1)}, u32[]{:S(2)}, u32[]{:S(2)}) %all-to-all-start.1) | async-done | bytes 3145760 | tf_op jit(solution)/shard_map/all_to_all | solution.py:252
  100.1 4.6 %regroup.4 = (bf16[6,512,256]{2,1,0:T(8,128)(2,1)}, bf16[6,512,256]{2,1,0:T(8,128)(2,1)}) custom-call(bf16[6144,256]{1,0:T(8,128)(2,1)} %bitcast.13.x_ref), custom_call_target="tpu_custom_call" | custom-call | flops 1207959552 | bytes 6291456 | tf_op jit(solution)/shard_map/regroup/pallas_call | solution.py:146
  105.6 4.4 %all-to-all-start.2 = ((bf16[32,24,1024]{2,1,0:T(8,128)(2,1)}), bf16[32,24,1024]{2,1,0:T(8,128)(2,1)S(1)}, u32[]{:S(2)}, u32[]{:S(2)}) async-start(bf16[32,24,1024]{2,1,0:T(8,128)(2,1)} %bitcast.45), calls=%async_computation.2 | async-start | bytes 3145728 | tf_op jit(solution)/shard_map/all_to_all | solution.py:252
  110.0 20.0 %collective-permute-done.1 = bf16[6,128,1024]{2,1,0:T(8,128)(2,1)} collective-permute-done((bf16[6,128,1024]{2,1,0:T(8,128)(2,1)S(1)}, bf16[6,128,1024]{2,1,0:T(8,128)(2,1)}, u32[]{:S(2)}, u32[]{:S(2)}) %collective-permute-start.1) | collective-permute-done | bytes 1572896 | tf_op jit(solution)/shard_map/ppermute | solution.py:242
  130.0 2.1 slice.17
  132.1 2.1 slice.16
  134.2 2.0 collective-permute-start.3
  136.5 21.2 %all-to-all-done.2 = bf16[32,24,1024]{2,1,0:T(8,128)(2,1)S(1)} async-done(((bf16[32,24,1024]{2,1,0:T(8,128)(2,1)}), bf16[32,24,1024]{2,1,0:T(8,128)(2,1)S(1)}, u32[]{:S(2)}, u32[]{:S(2)}) %all-to-all-start.2) | async-done | bytes 1572896 | tf_op jit(solution)/shard_map/all_to_all | solution.py:252
  157.7 1.3 regroup.5
  159.0 1.8 collective-permute-start.6
  161.8 29.6 %collective-permute-done.9 = bf16[6,512,256]{2,1,0:T(8,128)(2,1)} collective-permute-done((bf16[6,512,256]{2,1,0:T(8,128)(2,1)}, bf16[6,512,256]{2,1,0:T(8,128)(2,1)}, u32[]{:S(2)}, u32[]{:S(2)}) %collective-permute-start.9) | collective-permute-done | bytes 1572896 | tf_op jit(solution)/shard_map/ppermute | solution.py:245
  191.4 4.8 %collective-permute-done.6 = bf16[6,128,1024]{2,1,0:T(8,128)(2,1)S(1)} collective-permute-done((bf16[6,128,1024]{2,1,0:T(8,128)(2,1)S(1)}, bf16[6,128,1024]{2,1,0:T(8,128)(2,1)S(1)}, u32[]{:S(2)}, u32[]{:S(2)}) %collective-permute-start.6) | collective-permute-done | bytes 1572896 | tf_op jit(solution)/shard_map/ppermute | solution.py:242
  196.2 2.1 collective-permute-done.5
  202.6 1.3 collective-permute-start.7
  204.1 12.6 %correlate.2.refs_9_ = f32[6,2,512,512]{3,2,1,0:T(8,128)} custom-call(s32[8]{0:T(128)S(1)} %stack.40.order_ref, bf16[3,2,8,16,1024]{4,3,2,1,0:T(8,128)(2,1)S(1)} %bitcast.43, bf16[3,2,8,16,1024]{4,3,2,1,0:T(8,128)(2,1)} %bitcast.26.refs_1_, bf16[3,2,8,16,1024]{4,3,2,1,0:T(8,128)(2,1)} %bitcast.27.refs_2_, bf16[3,2,4,16,1024]{4,3,2,1,0:T(8,128)(2,1)} %bitcast.28.refs_3_, ...), custom_call_target="tpu_custom_call" | custom-call | flops 6442450944 | bytes 18874368 | tf_op jit(solution)/shard_map/correlate/pallas_call | solution.py:202
  216.7 2.8 %collective-permute-done.8 = bf16[6,64,1024]{2,1,0:T(8,128)(2,1)} collective-permute-done((bf16[6,64,1024]{2,1,0:T(8,128)(2,1)}, bf16[6,64,1024]{2,1,0:T(8,128)(2,1)}, u32[]{:S(2)}, u32[]{:S(2)}) %collective-permute-start.8) | collective-permute-done | bytes 786464 | tf_op jit(solution)/shard_map/ppermute | solution.py:242
  219.5 3.6 %collective-permute-done.7 = bf16[6,64,1024]{2,1,0:T(8,128)(2,1)} collective-permute-done((bf16[6,64,1024]{2,1,0:T(8,128)(2,1)}, bf16[6,64,1024]{2,1,0:T(8,128)(2,1)}, u32[]{:S(2)}, u32[]{:S(2)}) %collective-permute-start.7) | collective-permute-done | bytes 786464 | tf_op jit(solution)/shard_map/ppermute | solution.py:242
  223.1 12.5 %correlate.3 = f32[6,2,512,512]{3,2,1,0:T(8,128)} custom-call(s32[8]{0:T(128)S(1)} %stack.40.order_ref, bf16[3,2,8,16,1024]{4,3,2,1,0:T(8,128)(2,1)S(1)} %bitcast.40, bf16[3,2,8,16,1024]{4,3,2,1,0:T(8,128)(2,1)S(1)} %bitcast.44, bf16[3,2,8,16,1024]{4,3,2,1,0:T(8,128)(2,1)} %bitcast.47, ...), custom_call_target="tpu_custom_call", output_to_operand_aliasing={{}: (10, {})} | custom-call | flops 6442450944 | bytes 18874368 | tf_op jit(solution)/shard_map/correlate/pallas_call | solution.py:202
  (45 shorter events, 8.3 us)
Async XLA Ops:
  0.0 1.5 copy-start.7
  18.9 1.2 copy-start.4
  51.7 9.7 %copy-start = (bf16[6,128,1024]{2,1,0:T(8,128)(2,1)}, bf16[6,128,1024]{2,1,0:T(8,128)(2,1)S(1)}, u32[]{:S(2)}) copy-start(bf16[6,128,1024]{2,1,0:T(8,128)(2,1)S(1)} %regroup.3) | copy-start | bytes 4718596
  51.8 48.4 %all-to-all-start.1 = ((bf16[128,48,256]{2,1,0:T(8,128)(2,1)}), bf16[128,48,256]{2,1,0:T(8,128)(2,1)}, u32[]{:S(2)}, u32[]{:S(2)}) async-start(bf16[128,48,256]{2,1,0:T(8,128)(2,1)} %bitcast.48), calls=%async_computation.1 | async-start | bytes 6291456 | tf_op jit(solution)/shard_map/all_to_all | solution.py:252
  59.2 70.7 %collective-permute-start.1 = (bf16[6,128,1024]{2,1,0:T(8,128)(2,1)S(1)}, bf16[6,128,1024]{2,1,0:T(8,128)(2,1)}, u32[]{:S(2)}, u32[]{:S(2)}) collective-permute-start(bf16[6,128,1024]{2,1,0:T(8,128)(2,1)S(1)} %regroup.3), channel_id=1, source_target_pairs={{0,12},{4,0},{8,4},{12,8},{1,13},{5,1},{9,5},{13,9},{2,14},{6,2},{... | collective-permute-start | bytes 4718600 | tf_op jit(solution)/shard_map/ppermute | solution.py:242
  61.5 70.6 %collective-permute-start = (bf16[6,128,1024]{2,1,0:T(8,128)(2,1)S(1)}, bf16[6,128,1024]{2,1,0:T(8,128)(2,1)}, u32[]{:S(2)}, u32[]{:S(2)}) collective-permute-start(bf16[6,128,1024]{2,1,0:T(8,128)(2,1)S(1)} %regroup.3), channel_id=1, source_target_pairs={{0,4},{4,8},{8,12},{12,0},{1,5},{5,9},{9,13},{13,1},{2,6},{6,10},{... | collective-permute-start | bytes 4718600 | tf_op jit(solution)/shard_map/ppermute | solution.py:242
  104.7 53.0 %collective-permute-start.2 = (bf16[6,512,256]{2,1,0:T(8,128)(2,1)}, bf16[6,512,256]{2,1,0:T(8,128)(2,1)}, u32[]{:S(2)}, u32[]{:S(2)}) collective-permute-start(bf16[6,512,256]{2,1,0:T(8,128)(2,1)} %get-tuple-element.20), channel_id=1, source_target_pairs={{0,2},{2,0},{1,3},{3,1},{4,6},{6,4},{5,7},{7,5},{8,10},{10,8},{9,1... | collective-permute-start | bytes 4718600 | tf_op jit(solution)/shard_map/ppermute | solution.py:245
  105.6 52.1 %all-to-all-start.2 = ((bf16[32,24,1024]{2,1,0:T(8,128)(2,1)}), bf16[32,24,1024]{2,1,0:T(8,128)(2,1)S(1)}, u32[]{:S(2)}, u32[]{:S(2)}) async-start(bf16[32,24,1024]{2,1,0:T(8,128)(2,1)} %bitcast.45), calls=%async_computation.2 | async-start | bytes 3145728 | tf_op jit(solution)/shard_map/all_to_all | solution.py:252
  132.1 26.9 %collective-permute-start.4 = (bf16[6,64,1024]{2,1,0:T(8,128)(2,1)}, bf16[6,64,1024]{2,1,0:T(8,128)(2,1)}, u32[]{:S(2)}, u32[]{:S(2)}) collective-permute-start(bf16[6,64,1024]{2,1,0:T(8,128)(2,1)} %slice.17), channel_id=1, source_target_pairs={{0,12},{4,0},{8,4},{12,8},{1,13},{5,1},{9,5},{13,9},{2,14},{6,2},{... | collective-permute-start | bytes 2359304 | tf_op jit(solution)/shard_map/ppermute | solution.py:242
  134.2 24.9 %collective-permute-start.3 = (bf16[6,64,1024]{2,1,0:T(8,128)(2,1)}, bf16[6,64,1024]{2,1,0:T(8,128)(2,1)}, u32[]{:S(2)}, u32[]{:S(2)}) collective-permute-start(bf16[6,64,1024]{2,1,0:T(8,128)(2,1)} %slice.16), channel_id=1, source_target_pairs={{0,4},{4,8},{8,12},{12,0},{1,5},{5,9},{9,13},{13,1},{2,6},{6,10},{... | collective-permute-start | bytes 2359304 | tf_op jit(solution)/shard_map/ppermute | solution.py:242
  136.2 55.2 %collective-permute-start.9 = (bf16[6,512,256]{2,1,0:T(8,128)(2,1)}, bf16[6,512,256]{2,1,0:T(8,128)(2,1)}, u32[]{:S(2)}, u32[]{:S(2)}) collective-permute-start(bf16[6,512,256]{2,1,0:T(8,128)(2,1)} %get-tuple-element.25), channel_id=1, source_target_pairs={{0,2},{2,0},{1,3},{3,1},{4,6},{6,4},{5,7},{7,5},{8,10},{10,8},{9,1... | collective-permute-start | bytes 4718600 | tf_op jit(solution)/shard_map/ppermute | solution.py:245
  159.0 45.0 %copy-start.1 = (bf16[6,128,1024]{2,1,0:T(8,128)(2,1)S(1)}, bf16[6,128,1024]{2,1,0:T(8,128)(2,1)}, u32[]{:S(2)}) copy-start(bf16[6,128,1024]{2,1,0:T(8,128)(2,1)} %copy-done) | copy-start | bytes 4718596
  159.0 37.1 %collective-permute-start.6 = (bf16[6,128,1024]{2,1,0:T(8,128)(2,1)S(1)}, bf16[6,128,1024]{2,1,0:T(8,128)(2,1)S(1)}, u32[]{:S(2)}, u32[]{:S(2)}) collective-permute-start(bf16[6,128,1024]{2,1,0:T(8,128)(2,1)S(1)} %regroup.5), channel_id=1, source_target_pairs={{0,12},{4,0},{8,4},{12,8},{1,13},{5,1},{9,5},{13,9},{2,14},{6,2},{... | collective-permute-start | bytes 4718600 | tf_op jit(solution)/shard_map/ppermute | solution.py:242
  160.9 37.4 %collective-permute-start.5 = (bf16[6,128,1024]{2,1,0:T(8,128)(2,1)S(1)}, bf16[6,128,1024]{2,1,0:T(8,128)(2,1)S(1)}, u32[]{:S(2)}, u32[]{:S(2)}) collective-permute-start(bf16[6,128,1024]{2,1,0:T(8,128)(2,1)S(1)} %regroup.5), channel_id=1, source_target_pairs={{0,4},{4,8},{8,12},{12,0},{1,5},{5,9},{9,13},{13,1},{2,6},{6,10},{... | collective-permute-start | bytes 4718600 | tf_op jit(solution)/shard_map/ppermute | solution.py:242
  161.1 40.4 %collective-permute-start.12 = (bf16[6,512,256]{2,1,0:T(8,128)(2,1)}, bf16[6,512,256]{2,1,0:T(8,128)(2,1)S(1)}, u32[]{:S(2)}, u32[]{:S(2)}) collective-permute-start(bf16[6,512,256]{2,1,0:T(8,128)(2,1)} %get-tuple-element.20), channel_id=1, source_target_pairs={{0,1},{1,0},{2,3},{3,2},{4,5},{5,4},{6,7},{7,6},{8,9},{9,8},{10,11... | collective-permute-start | bytes 4718600 | tf_op jit(solution)/shard_map/ppermute | solution.py:245
  161.8 42.3 %collective-permute-start.13 = (bf16[6,512,256]{2,1,0:T(8,128)(2,1)}, bf16[6,512,256]{2,1,0:T(8,128)(2,1)}, u32[]{:S(2)}, u32[]{:S(2)}) collective-permute-start(bf16[6,512,256]{2,1,0:T(8,128)(2,1)} %collective-permute-done.2), channel_id=1, source_target_pairs={{0,1},{1,0},{2,3},{3,2},{4,5},{5,4},{6,7},{7,6},{8,9},{9,8},{10,11... | collective-permute-start | bytes 4718600 | tf_op jit(solution)/shard_map/ppermute | solution.py:245
  196.1 5.3 %copy-start.5 = (bf16[6,128,1024]{2,1,0:T(8,128)(2,1)}, bf16[6,128,1024]{2,1,0:T(8,128)(2,1)S(1)}, u32[]{:S(2)}) copy-start(bf16[6,128,1024]{2,1,0:T(8,128)(2,1)S(1)} %collective-permute-done.6) | copy-start | bytes 4718596
  198.2 3.3 %copy-start.2 = (bf16[6,128,1024]{2,1,0:T(8,128)(2,1)}, bf16[6,128,1024]{2,1,0:T(8,128)(2,1)S(1)}, u32[]{:S(2)}) copy-start(bf16[6,128,1024]{2,1,0:T(8,128)(2,1)S(1)} %collective-permute-done.5) | copy-start | bytes 4718596
  198.2 24.8 %collective-permute-start.10 = (bf16[6,512,256]{2,1,0:T(8,128)(2,1)}, bf16[6,512,256]{2,1,0:T(8,128)(2,1)}, u32[]{:S(2)}, u32[]{:S(2)}) collective-permute-start(bf16[6,512,256]{2,1,0:T(8,128)(2,1)} %get-tuple-element.25), channel_id=1, source_target_pairs={{0,1},{1,0},{2,3},{3,2},{4,5},{5,4},{6,7},{7,6},{8,9},{9,8},{10,11... | collective-permute-start | bytes 4718600 | tf_op jit(solution)/shard_map/ppermute | solution.py:245
  198.3 24.8 %collective-permute-start.11 = (bf16[6,512,256]{2,1,0:T(8,128)(2,1)}, bf16[6,512,256]{2,1,0:T(8,128)(2,1)}, u32[]{:S(2)}, u32[]{:S(2)}) collective-permute-start(bf16[6,512,256]{2,1,0:T(8,128)(2,1)} %collective-permute-done.9), channel_id=1, source_target_pairs={{0,1},{1,0},{2,3},{3,2},{4,5},{5,4},{6,7},{7,6},{8,9},{9,8},{10,11... | collective-permute-start | bytes 4718600 | tf_op jit(solution)/shard_map/ppermute | solution.py:245
  199.7 19.8 %collective-permute-start.8 = (bf16[6,64,1024]{2,1,0:T(8,128)(2,1)}, bf16[6,64,1024]{2,1,0:T(8,128)(2,1)}, u32[]{:S(2)}, u32[]{:S(2)}) collective-permute-start(bf16[6,64,1024]{2,1,0:T(8,128)(2,1)} %slice.19), channel_id=1, source_target_pairs={{0,12},{4,0},{8,4},{12,8},{1,13},{5,1},{9,5},{13,9},{2,14},{6,2},{... | collective-permute-start | bytes 2359304 | tf_op jit(solution)/shard_map/ppermute | solution.py:242
  201.5 1.1 copy-start.6
  202.6 20.4 %collective-permute-start.7 = (bf16[6,64,1024]{2,1,0:T(8,128)(2,1)}, bf16[6,64,1024]{2,1,0:T(8,128)(2,1)}, u32[]{:S(2)}, u32[]{:S(2)}) collective-permute-start(bf16[6,64,1024]{2,1,0:T(8,128)(2,1)} %slice.18), channel_id=1, source_target_pairs={{0,4},{4,8},{8,12},{12,0},{1,5},{5,9},{9,13},{13,1},{2,6},{6,10},{... | collective-permute-start | bytes 2359304 | tf_op jit(solution)/shard_map/ppermute | solution.py:242
  204.1 19.0 %copy-start.3 = (bf16[6,128,1024]{2,1,0:T(8,128)(2,1)S(1)}, bf16[6,128,1024]{2,1,0:T(8,128)(2,1)}, u32[]{:S(2)}) copy-start(bf16[6,128,1024]{2,1,0:T(8,128)(2,1)} %copy-done.2) | copy-start | bytes 4718596

commit v4 on v3

--- a/solution.py
+++ b/solution.py
@@ -174,16 +174,16 @@
             at = pl.multiple_of(order_ref[4 + k] * quarter, quarter)
             part = ref[0, plane]
             a_ref[:, pl.ds(plane * frames + at, quarter)] = part
-            if plane == 0:
-                a_ref[:, pl.ds(2 * frames + at, quarter)] = -part
     size = a_ref.shape[0]
     b = b_ref[...].reshape(size, 2 * frames)
     scale = 1.0 / frames
-    for plane in range(2):
-        a = a_ref[:, plane * frames : (plane + 2) * frames]
-        out_ref[0, plane] = (
-            lax.dot_general(a, b, (((1,), (1,)), ((), ())), preferred_element_type=F32) * scale
-        )
+
+    def cross(x, y):
+        return lax.dot_general(x, y, (((1,), (1,)), ((), ())), preferred_element_type=F32)
+
+    out_ref[0, 0] = cross(a_ref[...], b) * scale
+    imag = cross(a_ref[:, frames:], b[:, :frames]) - cross(a_ref[:, :frames], b[:, frames:])
+    out_ref[0, 1] = imag * scale
 
 
 def correlate(order, cols, pieces, out, first, total):
@@ -207,7 +207,7 @@
             in_specs=in_specs,
             out_specs=pl.BlockSpec((1, 2, size, size), lambda k, s: (first + k, 0, 0, 0)),
             scratch_shapes=[
-                pltpu.VMEM((size, 3 * frames), BF16),
+                pltpu.VMEM((size, 2 * frames), BF16),
                 pltpu.VMEM((chans, 4, rows_of, 2 * frames), BF16),
             ],
         ),

time: 236 us -> 236 us (level)
  no operation moved by 1% of the time
where the time goes in v4:
time: 236 us; the launch traced here: 235 us
  waiting for transfers between devices  123 us (52%)
  Pallas kernels  48.6 us (21%)
  blocking collectives  30.4 us (13%)
  starting transfers between devices  22.6 us (10%)
  local copies, waits for them, and re-layouts  9.65 us (4%)
    all_to_all x2, waiting for transfers between devices, exchange(): block = lax.all_to_all(block, axes, split_axis=0, concat_axis=0, tiled=True)  59.8 us
    ppermute x8, waiting for transfers between devices, turn(): lax.ppermute(x, 'row', [(k, (k + by) % row_count) for k in range(row_coun...  33.7 us
    all_to_all x1, blocking collectives, exchange(): block = lax.all_to_all(block, axes, split_axis=0, concat_axis=0, tiled=True)  30.4 us
    ppermute x6, waiting for transfers between devices, swap(): return lax.ppermute(x, axis, [(0, 1), (1, 0)])  29.6 us
    pallas_call x2, Pallas kernels, correlate(): pl.pallas_call(correlate_kernel, grid_spec=pltpu.PrefetchScalarGridSpec(n...  24.2 us
    pallas_call x1, Pallas kernels, spectra(): pl.pallas_call(spectra_kernel, grid=(panels,), in_specs=[pl.BlockSpec((2,...  17.2 us
    all_to_all x2, starting transfers between devices, exchange(): block = lax.all_to_all(block, axes, split_axis=0, concat_axis=0, tiled=True)  11.8 us
    ppermute x8, starting transfers between devices, turn(): lax.ppermute(x, 'row', [(k, (k + by) % row_count) for k in range(row_coun...  8.38 us
  transfers between devices with their start and end apart: 16, of which 8 were waited for; matrix products, arithmetic and copies ran while one was open for 3% of the time, Pallas kernels for 8%

profile of v4, /device:TPU:0, one launch (start us, length us, event | category | flops | bytes accessed | tf_op | source)
XLA Modules:
  0.0 235.1 jit_solution(280562904347907881)
XLA Ops:
  1.6 17.2 %spectra.1 = (bf16[8,4,24,1024]{3,2,1,0:T(8,128)(2,1)S(1)}, bf16[8,4,4,48,256]{4,3,2,1,0:T(8,128)(2,1)}, bf16[8,4,24,1024]{3,2,1,0:T(8,128)(2,1)S(1)}) custom-call(bf16[2,4,4,64,1031]{4,3,2,1,0:T(8,128)(2,1)} %volt_ref.1, f32[8,64,128]{2,1,0:T(8,128)S(1)} %broadcast_in_dim.2.win_ref, bf16[384,512]{1,0:T(8,128)(2,1)S(1)} %get-tuple-element.28.hi_ref, ...), custom_call_target="tpu_custom_call" | custom-call | tf_op jit(solution)/shard_map/spectra/pallas_call | solution.py:104
  18.9 1.2 copy-done.4
  20.0 30.4 %all_to_all.15 = bf16[32,24,1024]{2,1,0:T(8,128)(2,1)S(1)} all-to-all(bf16[32,24,1024]{2,1,0:T(8,128)(2,1)S(1)} %bitcast.46), channel_id=1, replica_groups=mesh['chan'=8,'row'=4,'col_0'=2,'col_1'=2] {'chan','col_0','col_1'}, dimensions={0} | all-to-all | bytes 3145728 | tf_op jit(solution)/shard_map/all_to_all | solution.py:252
  50.5 1.3 regroup.3
  51.8 7.5 %all-to-all-start.1 = ((bf16[128,48,256]{2,1,0:T(8,128)(2,1)}), bf16[128,48,256]{2,1,0:T(8,128)(2,1)}, u32[]{:S(2)}, u32[]{:S(2)}) async-start(bf16[128,48,256]{2,1,0:T(8,128)(2,1)} %bitcast.48), calls=%async_computation.1 | async-start | bytes 6291456 | tf_op jit(solution)/shard_map/all_to_all | solution.py:252
  59.2 2.2 collective-permute-start.1
  61.5 38.7 %all-to-all-done.1 = bf16[128,48,256]{2,1,0:T(8,128)(2,1)} async-done(((bf16[128,48,256]{2,1,0:T(8,128)(2,1)}), bf16[128,48,256]{2,1,0:T(8,128)(2,1)}, u32[]{:S(2)}, u32[]{:S(2)}) %all-to-all-start.1) | async-done | bytes 3145760 | tf_op jit(solution)/shard_map/all_to_all | solution.py:252
  100.1 4.6 %regroup.4 = (bf16[6,512,256]{2,1,0:T(8,128)(2,1)}, bf16[6,512,256]{2,1,0:T(8,128)(2,1)}) custom-call(bf16[6144,256]{1,0:T(8,128)(2,1)} %bitcast.13.x_ref), custom_call_target="tpu_custom_call" | custom-call | flops 1207959552 | bytes 6291456 | tf_op jit(solution)/shard_map/regroup/pallas_call | solution.py:146
  105.6 4.4 %all-to-all-start.2 = ((bf16[32,24,1024]{2,1,0:T(8,128)(2,1)}), bf16[32,24,1024]{2,1,0:T(8,128)(2,1)S(1)}, u32[]{:S(2)}, u32[]{:S(2)}) async-start(bf16[32,24,1024]{2,1,0:T(8,128)(2,1)} %bitcast.45), calls=%async_computation.2 | async-start | bytes 3145728 | tf_op jit(solution)/shard_map/all_to_all | solution.py:252
  110.0 20.0 %collective-permute-done.1 = bf16[6,128,1024]{2,1,0:T(8,128)(2,1)} collective-permute-done((bf16[6,128,1024]{2,1,0:T(8,128)(2,1)S(1)}, bf16[6,128,1024]{2,1,0:T(8,128)(2,1)}, u32[]{:S(2)}, u32[]{:S(2)}) %collective-permute-start.1) | collective-permute-done | bytes 1572896 | tf_op jit(solution)/shard_map/ppermute | solution.py:242
  130.0 2.1 slice.17
  132.1 2.1 slice.16
  134.2 2.0 collective-permute-start.3
  136.5 21.2 %all-to-all-done.2 = bf16[32,24,1024]{2,1,0:T(8,128)(2,1)S(1)} async-done(((bf16[32,24,1024]{2,1,0:T(8,128)(2,1)}), bf16[32,24,1024]{2,1,0:T(8,128)(2,1)S(1)}, u32[]{:S(2)}, u32[]{:S(2)}) %all-to-all-start.2) | async-done | bytes 1572896 | tf_op jit(solution)/shard_map/all_to_all | solution.py:252
  157.7 1.3 regroup.5
  159.0 1.8 collective-permute-start.6
  161.8 29.6 %collective-permute-done.9 = bf16[6,512,256]{2,1,0:T(8,128)(2,1)} collective-permute-done((bf16[6,512,256]{2,1,0:T(8,128)(2,1)}, bf16[6,512,256]{2,1,0:T(8,128)(2,1)}, u32[]{:S(2)}, u32[]{:S(2)}) %collective-permute-start.9) | collective-permute-done | bytes 1572896 | tf_op jit(solution)/shard_map/ppermute | solution.py:245
  191.4 4.8 %collective-permute-done.6 = bf16[6,128,1024]{2,1,0:T(8,128)(2,1)S(1)} collective-permute-done((bf16[6,128,1024]{2,1,0:T(8,128)(2,1)S(1)}, bf16[6,128,1024]{2,1,0:T(8,128)(2,1)S(1)}, u32[]{:S(2)}, u32[]{:S(2)}) %collective-permute-start.6) | collective-permute-done | bytes 1572896 | tf_op jit(solution)/shard_map/ppermute | solution.py:242
  196.2 2.1 collective-permute-done.5
  202.6 1.3 collective-permute-start.7
  204.1 12.2 %correlate.2.refs_9_ = f32[6,2,512,512]{3,2,1,0:T(8,128)} custom-call(s32[8]{0:T(128)S(1)} %stack.40.order_ref, bf16[3,2,8,16,1024]{4,3,2,1,0:T(8,128)(2,1)S(1)} %bitcast.43, bf16[3,2,8,16,1024]{4,3,2,1,0:T(8,128)(2,1)} %bitcast.26.refs_1_, bf16[3,2,8,16,1024]{4,3,2,1,0:T(8,128)(2,1)} %bitcast.27.refs_2_, bf16[3,2,4,16,1024]{4,3,2,1,0:T(8,128)(2,1)} %bitcast.28.refs_3_, ...), custom_call_target="tpu_custom_call" | custom-call | flops 6442450944 | bytes 18874368 | tf_op jit(solution)/shard_map/correlate/pallas_call | solution.py:202
  216.2 3.2 %collective-permute-done.8 = bf16[6,64,1024]{2,1,0:T(8,128)(2,1)} collective-permute-done((bf16[6,64,1024]{2,1,0:T(8,128)(2,1)}, bf16[6,64,1024]{2,1,0:T(8,128)(2,1)}, u32[]{:S(2)}, u32[]{:S(2)}) %collective-permute-start.8) | collective-permute-done | bytes 786464 | tf_op jit(solution)/shard_map/ppermute | solution.py:242
  219.5 3.6 %collective-permute-done.7 = bf16[6,64,1024]{2,1,0:T(8,128)(2,1)} collective-permute-done((bf16[6,64,1024]{2,1,0:T(8,128)(2,1)}, bf16[6,64,1024]{2,1,0:T(8,128)(2,1)}, u32[]{:S(2)}, u32[]{:S(2)}) %collective-permute-start.7) | collective-permute-done | bytes 786464 | tf_op jit(solution)/shard_map/ppermute | solution.py:242
  223.1 12.0 %correlate.3 = f32[6,2,512,512]{3,2,1,0:T(8,128)} custom-call(s32[8]{0:T(128)S(1)} %stack.40.order_ref, bf16[3,2,8,16,1024]{4,3,2,1,0:T(8,128)(2,1)S(1)} %bitcast.40, bf16[3,2,8,16,1024]{4,3,2,1,0:T(8,128)(2,1)S(1)} %bitcast.44, bf16[3,2,8,16,1024]{4,3,2,1,0:T(8,128)(2,1)} %bitcast.47, ...), custom_call_target="tpu_custom_call", output_to_operand_aliasing={{}: (10, {})} | custom-call | flops 6442450944 | bytes 18874368 | tf_op jit(solution)/shard_map/correlate/pallas_call | solution.py:202
  (45 shorter events, 8.3 us)
Async XLA Ops:
  0.0 1.5 copy-start.7
  18.9 1.2 copy-start.4
  51.7 9.7 %copy-start = (bf16[6,128,1024]{2,1,0:T(8,128)(2,1)}, bf16[6,128,1024]{2,1,0:T(8,128)(2,1)S(1)}, u32[]{:S(2)}) copy-start(bf16[6,128,1024]{2,1,0:T(8,128)(2,1)S(1)} %regroup.3) | copy-start | bytes 4718596
  51.8 48.4 %all-to-all-start.1 = ((bf16[128,48,256]{2,1,0:T(8,128)(2,1)}), bf16[128,48,256]{2,1,0:T(8,128)(2,1)}, u32[]{:S(2)}, u32[]{:S(2)}) async-start(bf16[128,48,256]{2,1,0:T(8,128)(2,1)} %bitcast.48), calls=%async_computation.1 | async-start | bytes 6291456 | tf_op jit(solution)/shard_map/all_to_all | solution.py:252
  59.2 70.7 %collective-permute-start.1 = (bf16[6,128,1024]{2,1,0:T(8,128)(2,1)S(1)}, bf16[6,128,1024]{2,1,0:T(8,128)(2,1)}, u32[]{:S(2)}, u32[]{:S(2)}) collective-permute-start(bf16[6,128,1024]{2,1,0:T(8,128)(2,1)S(1)} %regroup.3), channel_id=1, source_target_pairs={{0,12},{4,0},{8,4},{12,8},{1,13},{5,1},{9,5},{13,9},{2,14},{6,2},{... | collective-permute-start | bytes 4718600 | tf_op jit(solution)/shard_map/ppermute | solution.py:242
  61.5 70.6 %collective-permute-start = (bf16[6,128,1024]{2,1,0:T(8,128)(2,1)S(1)}, bf16[6,128,1024]{2,1,0:T(8,128)(2,1)}, u32[]{:S(2)}, u32[]{:S(2)}) collective-permute-start(bf16[6,128,1024]{2,1,0:T(8,128)(2,1)S(1)} %regroup.3), channel_id=1, source_target_pairs={{0,4},{4,8},{8,12},{12,0},{1,5},{5,9},{9,13},{13,1},{2,6},{6,10},{... | collective-permute-start | bytes 4718600 | tf_op jit(solution)/shard_map/ppermute | solution.py:242
  104.7 53.0 %collective-permute-start.2 = (bf16[6,512,256]{2,1,0:T(8,128)(2,1)}, bf16[6,512,256]{2,1,0:T(8,128)(2,1)}, u32[]{:S(2)}, u32[]{:S(2)}) collective-permute-start(bf16[6,512,256]{2,1,0:T(8,128)(2,1)} %get-tuple-element.20), channel_id=1, source_target_pairs={{0,2},{2,0},{1,3},{3,1},{4,6},{6,4},{5,7},{7,5},{8,10},{10,8},{9,1... | collective-permute-start | bytes 4718600 | tf_op jit(solution)/shard_map/ppermute | solution.py:245
  105.6 52.1 %all-to-all-start.2 = ((bf16[32,24,1024]{2,1,0:T(8,128)(2,1)}), bf16[32,24,1024]{2,1,0:T(8,128)(2,1)S(1)}, u32[]{:S(2)}, u32[]{:S(2)}) async-start(bf16[32,24,1024]{2,1,0:T(8,128)(2,1)} %bitcast.45), calls=%async_computation.2 | async-start | bytes 3145728 | tf_op jit(solution)/shard_map/all_to_all | solution.py:252
  132.1 26.9 %collective-permute-start.4 = (bf16[6,64,1024]{2,1,0:T(8,128)(2,1)}, bf16[6,64,1024]{2,1,0:T(8,128)(2,1)}, u32[]{:S(2)}, u32[]{:S(2)}) collective-permute-start(bf16[6,64,1024]{2,1,0:T(8,128)(2,1)} %slice.17), channel_id=1, source_target_pairs={{0,12},{4,0},{8,4},{12,8},{1,13},{5,1},{9,5},{13,9},{2,14},{6,2},{... | collective-permute-start | bytes 2359304 | tf_op jit(solution)/shard_map/ppermute | solution.py:242
  134.2 24.9 %collective-permute-start.3 = (bf16[6,64,1024]{2,1,0:T(8,128)(2,1)}, bf16[6,64,1024]{2,1,0:T(8,128)(2,1)}, u32[]{:S(2)}, u32[]{:S(2)}) collective-permute-start(bf16[6,64,1024]{2,1,0:T(8,128)(2,1)} %slice.16), channel_id=1, source_target_pairs={{0,4},{4,8},{8,12},{12,0},{1,5},{5,9},{9,13},{13,1},{2,6},{6,10},{... | collective-permute-start | bytes 2359304 | tf_op jit(solution)/shard_map/ppermute | solution.py:242
  136.2 55.2 %collective-permute-start.9 = (bf16[6,512,256]{2,1,0:T(8,128)(2,1)}, bf16[6,512,256]{2,1,0:T(8,128)(2,1)}, u32[]{:S(2)}, u32[]{:S(2)}) collective-permute-start(bf16[6,512,256]{2,1,0:T(8,128)(2,1)} %get-tuple-element.25), channel_id=1, source_target_pairs={{0,2},{2,0},{1,3},{3,1},{4,6},{6,4},{5,7},{7,5},{8,10},{10,8},{9,1... | collective-permute-start | bytes 4718600 | tf_op jit(solution)/shard_map/ppermute | solution.py:245
  159.0 45.0 %copy-start.1 = (bf16[6,128,1024]{2,1,0:T(8,128)(2,1)S(1)}, bf16[6,128,1024]{2,1,0:T(8,128)(2,1)}, u32[]{:S(2)}) copy-start(bf16[6,128,1024]{2,1,0:T(8,128)(2,1)} %copy-done) | copy-start | bytes 4718596
  159.0 37.1 %collective-permute-start.6 = (bf16[6,128,1024]{2,1,0:T(8,128)(2,1)S(1)}, bf16[6,128,1024]{2,1,0:T(8,128)(2,1)S(1)}, u32[]{:S(2)}, u32[]{:S(2)}) collective-permute-start(bf16[6,128,1024]{2,1,0:T(8,128)(2,1)S(1)} %regroup.5), channel_id=1, source_target_pairs={{0,12},{4,0},{8,4},{12,8},{1,13},{5,1},{9,5},{13,9},{2,14},{6,2},{... | collective-permute-start | bytes 4718600 | tf_op jit(solution)/shard_map/ppermute | solution.py:242
  160.9 37.4 %collective-permute-start.5 = (bf16[6,128,1024]{2,1,0:T(8,128)(2,1)S(1)}, bf16[6,128,1024]{2,1,0:T(8,128)(2,1)S(1)}, u32[]{:S(2)}, u32[]{:S(2)}) collective-permute-start(bf16[6,128,1024]{2,1,0:T(8,128)(2,1)S(1)} %regroup.5), channel_id=1, source_target_pairs={{0,4},{4,8},{8,12},{12,0},{1,5},{5,9},{9,13},{13,1},{2,6},{6,10},{... | collective-permute-start | bytes 4718600 | tf_op jit(solution)/shard_map/ppermute | solution.py:242
  161.1 40.4 %collective-permute-start.12 = (bf16[6,512,256]{2,1,0:T(8,128)(2,1)}, bf16[6,512,256]{2,1,0:T(8,128)(2,1)S(1)}, u32[]{:S(2)}, u32[]{:S(2)}) collective-permute-start(bf16[6,512,256]{2,1,0:T(8,128)(2,1)} %get-tuple-element.20), channel_id=1, source_target_pairs={{0,1},{1,0},{2,3},{3,2},{4,5},{5,4},{6,7},{7,6},{8,9},{9,8},{10,11... | collective-permute-start | bytes 4718600 | tf_op jit(solution)/shard_map/ppermute | solution.py:245
  161.8 42.3 %collective-permute-start.13 = (bf16[6,512,256]{2,1,0:T(8,128)(2,1)}, bf16[6,512,256]{2,1,0:T(8,128)(2,1)}, u32[]{:S(2)}, u32[]{:S(2)}) collective-permute-start(bf16[6,512,256]{2,1,0:T(8,128)(2,1)} %collective-permute-done.2), channel_id=1, source_target_pairs={{0,1},{1,0},{2,3},{3,2},{4,5},{5,4},{6,7},{7,6},{8,9},{9,8},{10,11... | collective-permute-start | bytes 4718600 | tf_op jit(solution)/shard_map/ppermute | solution.py:245
  196.1 5.3 %copy-start.5 = (bf16[6,128,1024]{2,1,0:T(8,128)(2,1)}, bf16[6,128,1024]{2,1,0:T(8,128)(2,1)S(1)}, u32[]{:S(2)}) copy-start(bf16[6,128,1024]{2,1,0:T(8,128)(2,1)S(1)} %collective-permute-done.6) | copy-start | bytes 4718596
  198.2 3.3 %copy-start.2 = (bf16[6,128,1024]{2,1,0:T(8,128)(2,1)}, bf16[6,128,1024]{2,1,0:T(8,128)(2,1)S(1)}, u32[]{:S(2)}) copy-start(bf16[6,128,1024]{2,1,0:T(8,128)(2,1)S(1)} %collective-permute-done.5) | copy-start | bytes 4718596
  198.2 24.8 %collective-permute-start.10 = (bf16[6,512,256]{2,1,0:T(8,128)(2,1)}, bf16[6,512,256]{2,1,0:T(8,128)(2,1)}, u32[]{:S(2)}, u32[]{:S(2)}) collective-permute-start(bf16[6,512,256]{2,1,0:T(8,128)(2,1)} %get-tuple-element.25), channel_id=1, source_target_pairs={{0,1},{1,0},{2,3},{3,2},{4,5},{5,4},{6,7},{7,6},{8,9},{9,8},{10,11... | collective-permute-start | bytes 4718600 | tf_op jit(solution)/shard_map/ppermute | solution.py:245
  198.3 24.8 %collective-permute-start.11 = (bf16[6,512,256]{2,1,0:T(8,128)(2,1)}, bf16[6,512,256]{2,1,0:T(8,128)(2,1)}, u32[]{:S(2)}, u32[]{:S(2)}) collective-permute-start(bf16[6,512,256]{2,1,0:T(8,128)(2,1)} %collective-permute-done.9), channel_id=1, source_target_pairs={{0,1},{1,0},{2,3},{3,2},{4,5},{5,4},{6,7},{7,6},{8,9},{9,8},{10,11... | collective-permute-start | bytes 4718600 | tf_op jit(solution)/shard_map/ppermute | solution.py:245
  199.7 19.8 %collective-permute-start.8 = (bf16[6,64,1024]{2,1,0:T(8,128)(2,1)}, bf16[6,64,1024]{2,1,0:T(8,128)(2,1)}, u32[]{:S(2)}, u32[]{:S(2)}) collective-permute-start(bf16[6,64,1024]{2,1,0:T(8,128)(2,1)} %slice.19), channel_id=1, source_target_pairs={{0,12},{4,0},{8,4},{12,8},{1,13},{5,1},{9,5},{13,9},{2,14},{6,2},{... | collective-permute-start | bytes 2359304 | tf_op jit(solution)/shard_map/ppermute | solution.py:242
  201.5 1.1 copy-start.6
  202.6 20.4 %collective-permute-start.7 = (bf16[6,64,1024]{2,1,0:T(8,128)(2,1)}, bf16[6,64,1024]{2,1,0:T(8,128)(2,1)}, u32[]{:S(2)}, u32[]{:S(2)}) collective-permute-start(bf16[6,64,1024]{2,1,0:T(8,128)(2,1)} %slice.18), channel_id=1, source_target_pairs={{0,4},{4,8},{8,12},{12,0},{1,5},{5,9},{9,13},{13,1},{2,6},{6,10},{... | collective-permute-start | bytes 2359304 | tf_op jit(solution)/shard_map/ppermute | solution.py:242
  204.1 19.0 %copy-start.3 = (bf16[6,128,1024]{2,1,0:T(8,128)(2,1)S(1)}, bf16[6,128,1024]{2,1,0:T(8,128)(2,1)}, u32[]{:S(2)}) copy-start(bf16[6,128,1024]{2,1,0:T(8,128)(2,1)} %copy-done.2) | copy-start | bytes 4718596
